TPU v7x, 32 devices: a whole 2x2x4 slice. The times are simulated.
32 devices in a mesh: team: 2 (over core), obs: 4 (over z), grid: 4 (over y, x).
Axes of the slice: x: 2, y: 2, z: 4, core: 2. Of those that a mesh axis runs over, the one named last changes fastest.
Arguments:
- design_panel: bfloat16 [8192, 1024], P('obs', ('team', 'grid')), may hold values from -6 to 6
- design_front: bfloat16 [8192, 6144], P('obs', 'grid'), may hold values from -6 to 6
- arc_ids: int32 [8192], P('obs'), may hold values from 0 to 127
- arc_weight: float32 [128], replicated, may hold values from 0.5 to 2
- row_counts: int32 [4], P('obs'), may hold values from 128 to 2048, as said below
- panel_inverse: float32 [1024, 1024], P(('team', 'obs')), may hold values from -6.525546e-05 to 0.0020539933
- front: float32 [6144, 6144], P(('team', 'obs'), 'grid'), may hold values from -1.2 to 21.2
Outputs:
- factor_row: float32 [1024, 6144], P(('team', 'obs'), 'grid')
- front_next: float32 [6144, 6144], P(('team', 'obs'), 'grid')
Inputs may be any that keep to these rules, and one draw needn't show every extreme that they name: `row_counts`: every count is a multiple of 128, and in every draw some shard's count equals 2048.
All inputs are finite; a program needn't handle non-finite values.
Results may differ from a plain program's by a relative error of at most 0.0035.
Values may be sent and summed in bfloat16 or wider, within the bound.
A program may use at most 64 MiB of HBM per device.

v0:
```python
import functools

import jax
import jax.numpy as jnp
from jax import lax
from jax.experimental import pallas as pl
from jax.experimental.pallas import tpu as pltpu
from jax.sharding import PartitionSpec as P


def live_weights(arc_ids, arc_weight, row_counts):
    row_total = arc_ids.shape[0]
    arc_total = arc_weight.shape[0]
    hit = arc_ids[:, None] == lax.broadcasted_iota(jnp.int32, (row_total, arc_total), 1)
    looked = jnp.sum(jnp.where(hit, arc_weight[None, :], 0.0), axis=1)
    is_live = lax.broadcasted_iota(jnp.int32, (row_total,), 0) < row_counts[0]
    return looked * is_live.astype(jnp.float32)


def contract_rows(left, right):
    return lax.dot_general(
        left, right, (((0,), (0,)), ((), ())), preferred_element_type=jnp.float32
    )


def local(design_panel, design_front, arc_ids, arc_weight, row_counts, panel_inverse, front):
    high = lax.reduce_precision(panel_inverse, 8, 7)
    split = jnp.concatenate([high, panel_inverse - high], axis=1).astype(jnp.bfloat16)
    inverse_whole = lax.all_gather(split, ("team", "obs"), axis=0, tiled=True)
    weights = live_weights(arc_ids, arc_weight, row_counts)
    scaled_front = (design_front.astype(jnp.float32) * weights[:, None]).astype(jnp.bfloat16)
    panel_piece = lax.all_gather(design_panel, "grid", axis=1, tiled=True)
    partial_value = contract_rows(panel_piece, scaled_front)
    slab_rows = panel_inverse.shape[0]
    place_index = lax.axis_index(("team", "obs"))
    block_part = lax.psum_scatter(partial_value, "obs", scatter_dimension=0, tiled=True)
    block_part = block_part.astype(jnp.bfloat16)
    block_whole = lax.all_gather(block_part, ("team", "obs"), axis=0, tiled=True)
    factor_cols = jnp.dot(
        inverse_whole,
        jnp.concatenate([block_whole, block_whole], axis=0),
        preferred_element_type=jnp.float32,
    )
    factor_part = lax.dynamic_slice_in_dim(factor_cols, place_index * slab_rows, slab_rows, 0)
    factor_cols = factor_cols.astype(jnp.bfloat16)
    tile_rows = front.shape[0]
    tile_ratio = factor_cols.shape[1] // tile_rows
    offset = place_index % tile_ratio * tile_rows
    own_slice = lax.dynamic_slice_in_dim(factor_cols, offset, tile_rows, 1)
    kept = jnp.where(lax.axis_index("grid") == place_index // tile_ratio, own_slice, 0)
    factor_rows = lax.psum(kept.astype(jnp.bfloat16), "grid")
    return (factor_part, front - contract_rows(factor_rows, factor_cols))


MESH = pl.DeviceIdType.MESH


def exchange(
    ratio, panel, front_cols, weights, inverse_rows,
    blk, tile, inv,
    panels, scaled, outgoing, incoming, own_sum,
    local_sem, panel_send, panel_recv, sum_send, sum_recv,
    line_send, line_recv, inv_send, inv_recv,
    team_send, team_recv, inv_team_send, inv_team_recv, inv_grid_send, inv_grid_recv, tile_send, tile_recv,
):
    team, z, grid = lax.axis_index("team"), lax.axis_index("obs"), lax.axis_index("grid")
    lines = blk.shape[2]
    groups = blk.shape[1]
    x, y = lax.rem(grid, 2), lax.div(grid, 2)
    beside_x = y * 2 + (1 - x)
    beside_y = (1 - y) * 2 + x
    across = (1 - y) * 2 + (1 - x)
    partner = 1 - team
    place = team * lines + z
    root, half = lax.div(place, ratio), lax.rem(place, ratio)
    per_half = lines // ratio
    root_x, root_y = lax.rem(root, 2), lax.div(root, 2)
    is_root = grid == root
    is_relay = grid == root_y * 2 + (1 - root_x)
    width = panel.shape[1]
    piece = scaled.shape[2]

    barrier = pltpu.get_barrier_semaphore()
    for peer in (beside_x, beside_y, across):
        pl.semaphore_signal(barrier, inc=1, device_id={"grid": peer}, device_id_type=MESH)
    for p in range(1, lines):
        pl.semaphore_signal(
            barrier, inc=1, device_id={"obs": lax.rem(z + p, lines)}, device_id_type=MESH
        )
    pl.semaphore_signal(barrier, inc=1, device_id={"team": partner}, device_id_type=MESH)
    pl.semaphore_wait(barrier, lines + 3)

    def remote(src, dst, send, recv, where):
        return pltpu.make_async_remote_copy(
            src_ref=src, dst_ref=dst, send_sem=send, recv_sem=recv,
            device_id=where, device_id_type=MESH,
        )

    def panel_slot(index):
        return panels.at[lax.div(index, 2), :, pl.ds(pl.multiple_of(lax.rem(index, 2) * width, width), width)]

    panel_copies = []
    for k, peer in enumerate((beside_x, beside_y)):
        panel_copies.append(
            remote(panel, panel_slot(grid), panel_send.at[k], panel_recv.at[k], {"grid": peer})
        )
        panel_copies[-1].start()
    rows = panel.shape[0]
    middle = rows // 2
    for k, (source, peer) in enumerate(((beside_x, beside_y), (beside_y, beside_x))):
        cut = panel_slot(source).at[pl.ds(k * middle, middle)]
        panel_copies.append(
            remote(cut, cut, panel_send.at[2 + k], panel_recv.at[2 + k], {"grid": peer})
        )
    own_panel = pltpu.make_async_copy(panel, panel_slot(grid), local_sem.at[0])
    own_panel.start()
    share = inv.shape[3]
    own_rows = inverse_rows.at[pl.ds(pl.multiple_of(grid * share, share), share)]
    own_inv = pltpu.make_async_copy(own_rows, inv.at[team, z, grid], local_sem.at[1])
    own_inv.start()

    def line_sends(ref_of, send, recv, s):
        for d, step in ((0, 1), (1, -1)):
            held = z - step * s
            ok = (held >= 0) & (held < lines) & (z + step >= 0) & (z + step < lines)
            idx = jnp.clip(held, 0, lines - 1)
            nxt = jnp.clip(z + step, 0, lines - 1)

            @pl.when(ok)
            def _():
                remote(ref_of(idx), ref_of(idx), send.at[d, s], recv.at[d, s], {"obs": nxt}).start()

    def line_waits(ref_of, send, recv, s, then):
        for d, step in ((0, 1), (1, -1)):
            came = z - step * (s + 1)

            @pl.when((came >= 0) & (came < lines))
            def _():
                idx = jnp.clip(came, 0, lines - 1)
                pltpu.make_async_copy(ref_of(idx), ref_of(idx), recv.at[d, s]).wait()
                then(idx)

    def line_drain(ref_of, send):
        for s in range(lines - 1):
            for d, step in ((0, 1), (1, -1)):
                held = z - step * s

                @pl.when((held >= 0) & (held < lines) & (z + step >= 0) & (z + step < lines))
                def _():
                    idx = jnp.clip(held, 0, lines - 1)
                    pltpu.make_async_copy(ref_of(idx), ref_of(idx), send.at[d, s]).wait()

    def inv_of(idx):
        return inv.at[team, idx, grid]

    def nothing(idx):
        pass

    own_inv.wait()
    line_sends(inv_of, inv_send, inv_recv, 0)

    step_rows = 256

    @pl.loop(0, rows // step_rows)
    def _(i):
        at = pl.ds(pl.multiple_of(i * step_rows, step_rows), step_rows)
        factor = weights[at, :]
        for q in range(lines):
            part = front_cols[at, q * piece:(q + 1) * piece].astype(jnp.float32)
            scaled[q, at, :] = (part * factor).astype(jnp.bfloat16)

    own_panel.wait()
    sum_copies = []
    for order in range(groups):
        g = y if order == 0 else 1 - y
        if order == 0:
            for s in range(lines - 2):
                line_waits(inv_of, inv_send, inv_recv, s, nothing)
                line_sends(inv_of, inv_send, inv_recv, s + 1)
            panel_copies[0].wait_recv()
            panel_copies[2].start()
            panel_copies[1].wait_recv()
            panel_copies[3].start()
        else:
            panel_copies[2].wait_recv()
            panel_copies[3].wait_recv()
        for p in (2, 1, 3, 0):
            dest = lax.rem(z + p, lines)
            total = contract_rows(panels[g], scaled[dest])
            if p == 0:
                own_sum[order] = total
            else:
                outgoing[order, p - 1] = total.astype(jnp.bfloat16)
                copy = remote(
                    outgoing.at[order, p - 1], incoming.at[order, p - 1],
                    sum_send.at[order, p - 1], sum_recv.at[order, p - 1], {"obs": dest},
                )
                copy.start()
                sum_copies.append(copy)

    line_waits(inv_of, inv_send, inv_recv, lines - 2, nothing)
    inv_copies = []
    for k, peer in enumerate((beside_x, beside_y, across)):
        own = inv.at[team, :, grid]
        inv_copies.append(remote(own, own, inv_grid_send.at[k], inv_grid_recv.at[k], {"grid": peer}))
        inv_copies[-1].start()

    def finished(t, g, order, idx):
        @pl.when(is_root & (lax.div(idx, per_half) == half))
        def _():
            q = lax.rem(idx, per_half)
            for k, peer in ((0, beside_x), (1, beside_y)):
                remote(blk.at[t, g, idx], tile.at[t, g, q], tile_send.at[k, t, g, q],
                       tile_recv.at[t, g, q], {"grid": peer}).start()
            pltpu.make_async_copy(blk.at[t, g, idx], tile.at[t, g, q], tile_recv.at[t, g, q]).start()

    def line_done(g, order, idx):
        remote(blk.at[team, g, idx], blk.at[team, g, idx], team_send.at[g, idx],
               team_recv.at[g, idx], {"team": partner}).start()
        finished(team, g, order, idx)

    for order in range(groups):
        g = y if order == 0 else 1 - y
        total = own_sum[order]
        for p in (1, 3, 2):
            sum_copies[order * (lines - 1) + (2, 1, 3).index(p)].wait_recv()
            total = total + incoming[order, p - 1].astype(jnp.float32)
        blk[team, g, z] = total.astype(jnp.bfloat16)

        def of(idx, g=g):
            return blk.at[team, g, idx]

        line_sends(of, line_send.at[order], line_recv.at[order], 0)
        line_done(g, order, z)

    def settle(idx):
        for order in range(groups):
            g = y if order == 0 else 1 - y
            pltpu.make_async_copy(
                blk.at[partner, g, idx], blk.at[partner, g, idx], team_recv.at[g, idx]
            ).wait()
            finished(partner, g, order, idx)

    def relay(idx):
        for t in (team, partner):
            for order in range(groups):
                g = y if order == 0 else 1 - y

                @pl.when(is_relay & (lax.div(idx, per_half) == half))
                def _():
                    q = lax.rem(idx, per_half)
                    dst = tile.at[t, g, q]
                    pltpu.make_async_copy(dst, dst, tile_recv.at[t, g, q]).wait()
                    remote(dst, dst, tile_send.at[0, t, g, q], tile_recv.at[t, g, q],
                           {"grid": beside_y}).start()

    def each_at(s, then):
        if s < 0:
            then(z)
            return
        for step in (1, -1):
            came = z - step * (s + 1)

            @pl.when((came >= 0) & (came < lines))
            def _():
                then(jnp.clip(came, 0, lines - 1))

    for s in range(lines - 1):
        for order in range(groups):
            g = y if order == 0 else 1 - y

            def of(idx, g=g):
                return blk.at[team, g, idx]

            line_waits(of, line_send.at[order], line_recv.at[order], s,
                       lambda idx: line_done(g, order, idx))
            if s + 1 < lines - 1:
                line_sends(of, line_send.at[order], line_recv.at[order], s + 1)
        if s == 0:
            for copy in inv_copies:
                copy.wait_recv()
            inv_team = remote(inv.at[team], inv.at[team], inv_team_send, inv_team_recv, {"team": partner})
            inv_team.start()
        each_at(s - 1, settle)
        if s > 0:
            each_at(s - 2, relay)
    each_at(lines - 2, settle)
    each_at(lines - 3, relay)
    each_at(lines - 2, relay)

    for t in (team, partner):
        for order in range(groups):
            g = y if order == 0 else 1 - y
            for q in range(per_half):
                dst = tile.at[t, g, q]

                @pl.when(jnp.logical_not(is_relay))
                def _():
                    pltpu.make_async_copy(dst, dst, tile_recv.at[t, g, q]).wait()

    inv_team.wait()
    for copy in panel_copies + sum_copies + inv_copies:
        copy.wait_send()
    line_drain(inv_of, inv_send)
    for order in range(groups):
        g = y if order == 0 else 1 - y
        line_drain(lambda idx: blk.at[team, g, idx], line_send.at[order])
    for idx in range(lines):
        for g in range(groups):
            ref = blk.at[team, g, idx]
            pltpu.make_async_copy(ref, ref, team_send.at[g, idx]).wait()
    for t in range(2):
        for g in range(groups):
            for q in range(per_half):
                ref = tile.at[t, g, q]

                @pl.when(is_root | is_relay)
                def _():
                    pltpu.make_async_copy(ref, ref, tile_send.at[0, t, g, q]).wait()

                @pl.when(is_root)
                def _():
                    pltpu.make_async_copy(ref, ref, tile_send.at[1, t, g, q]).wait()


def finish(spot, blk, tile, inv, front, factor_out, front_out, cols, high, low, held, sems):
    pieces, blocks, size = blk.shape[1], blk.shape[0], blk.shape[2]
    piece = blk.shape[3]
    whole = blocks * size
    slab = factor_out.shape[0]

    load = pltpu.make_async_copy(front, held, sems.at[0])
    load.start()

    def factor_of(source, q, r):
        total = inv[r * size:(r + 1) * size, whole:whole + 1].astype(jnp.float32)
        total = total * source[r, q].astype(jnp.float32)
        for k in range(r + 1):
            total += jnp.dot(
                inv[r * size:(r + 1) * size, k * size:(k + 1) * size], source[k, q],
                preferred_element_type=jnp.float32,
            )
        return total

    for r in range(blocks):
        for q in range(pieces):
            value = factor_of(blk, q, r)
            cols[q, r * size:(r + 1) * size, :] = value.astype(jnp.bfloat16)
            for part in range(size // slab):
                @pl.when(spot[0] == r * (size // slab) + part)
                def _():
                    factor_out[:, q * piece:(q + 1) * piece] = value[part * slab:(part + 1) * slab]
        for q in range(tile.shape[1]):
            value = factor_of(tile, q, r)
            value = value.T
            top = value.astype(jnp.bfloat16)
            high[q, :, r * size:(r + 1) * size] = top
            low[q, :, r * size:(r + 1) * size] = (value - top.astype(jnp.float32)).astype(jnp.bfloat16)

    load.wait()
    stores = []
    for h in range(tile.shape[1]):
        for q in range(pieces):
            update = jnp.dot(high[h], cols[q], preferred_element_type=jnp.float32)
            update += jnp.dot(low[h], cols[q], preferred_element_type=jnp.float32)
            at = (pl.ds(h * piece, piece), pl.ds(q * piece, piece))
            held[at] = held[at] - update
            stores.append(
                pltpu.make_async_copy(held.at[at], front_out.at[at], sems.at[1 + h * pieces + q])
            )
            stores[-1].start()
    for store in stores:
        store.wait()


def local_kernels(lines, grids, design_panel, design_front, arc_ids, arc_weight, row_counts, panel_inverse, front):
    bf16 = jnp.bfloat16
    weights = live_weights(arc_ids, arc_weight, row_counts)[:, None]
    slab, whole = panel_inverse.shape
    rows, width = design_panel.shape
    cols = design_front.shape[1]
    tile_rows = front.shape[0]
    ratio = cols // tile_rows
    piece = cols // lines
    groups = 2
    size = 2 * width
    place = lax.axis_index(("team", "obs"))
    top = lax.reduce_precision(panel_inverse, 8, 7)
    row_at = lax.broadcasted_iota(jnp.int32, (slab, whole), 0) + place * slab
    on_diagonal = lax.broadcasted_iota(jnp.int32, (slab, whole), 1) == row_at
    rest = jnp.sum(jnp.where(on_diagonal, panel_inverse - top, 0.0), axis=1, keepdims=True)
    inverse_rows = jnp.concatenate(
        [top, jnp.broadcast_to(rest, (slab, 128))], axis=1
    ).astype(bf16)
    vmem = pl.BlockSpec(memory_space=pltpu.VMEM)
    dma = pltpu.SemaphoreType.DMA
    hops = lines - 1
    halves = lines // ratio
    blk, tile, inv = pl.pallas_call(
        functools.partial(exchange, ratio),
        out_shape=(
            jax.ShapeDtypeStruct((2, groups, lines, size, piece), bf16),
            jax.ShapeDtypeStruct((2, groups, halves, size, piece), bf16),
            jax.ShapeDtypeStruct((2, lines, grids, slab // grids, inverse_rows.shape[1]), bf16),
        ),
        in_specs=[vmem] * 4,
        out_specs=(vmem,) * 3,
        scratch_shapes=[
            pltpu.VMEM((groups, rows, size), bf16),
            pltpu.VMEM((lines, rows, piece), bf16),
            pltpu.VMEM((groups, hops, size, piece), bf16),
            pltpu.VMEM((groups, hops, size, piece), bf16),
            pltpu.VMEM((groups, size, piece), jnp.float32),
            dma((2,)), dma((4,)), dma((4,)),
            dma((groups, hops)), dma((groups, hops)),
            dma((groups, 2, hops)), dma((groups, 2, hops)),
            dma((2, hops)), dma((2, hops)),
            dma((groups, lines)), dma((groups, lines)),
            dma, dma, dma((3,)), dma((3,)),
            dma((2, 2, groups, halves)), dma((2, groups, halves)),
        ],
        compiler_params=pltpu.CompilerParams(
            collective_id=0, has_side_effects=True, vmem_limit_bytes=48 * 2**20
        ),
        name="exchange",
    )(design_panel, design_front, weights, inverse_rows)
    blk = blk.reshape((2 * groups, lines, size, piece))
    tile = tile.reshape((2 * groups, halves, size, piece))
    inv = inv.reshape((whole, inverse_rows.shape[1]))
    return pl.pallas_call(
        finish,
        out_shape=(
            jax.ShapeDtypeStruct((slab, cols), jnp.float32),
            jax.ShapeDtypeStruct(front.shape, jnp.float32),
        ),
        in_specs=[pl.BlockSpec(memory_space=pltpu.SMEM)] + [vmem] * 3 + [pl.BlockSpec(memory_space=pl.ANY)],
        out_specs=(vmem, pl.BlockSpec(memory_space=pl.ANY)),
        scratch_shapes=[
            pltpu.VMEM((lines, whole, piece), bf16),
            pltpu.VMEM((halves, piece, whole), bf16),
            pltpu.VMEM((halves, piece, whole), bf16),
            pltpu.VMEM(front.shape, jnp.float32),
            dma((1 + halves * lines,)),
        ],
        compiler_params=pltpu.CompilerParams(vmem_limit_bytes=48 * 2**20),
        name="finish",
    )(place.astype(jnp.int32)[None], blk, tile, inv, front)


def solution(mesh):
    placed = (
        P("obs", ("team", "grid")),
        P("obs", "grid"),
        P("obs"),
        P(),
        P("obs"),
        P(("team", "obs"), None),
        P(("team", "obs"), "grid"),
    )
    sizes = mesh.shape
    fits = sizes["team"] == 2 and sizes["obs"] == 4 and sizes["grid"] == 4
    return jax.shard_map(
        functools.partial(local_kernels, sizes["obs"], sizes["grid"]) if fits else local,
        mesh=mesh,
        in_specs=placed,
        out_specs=(P(("team", "obs"), "grid"), P(("team", "obs"), "grid")),
        check_vma=False,
    )
```

profile of v0, /device:TPU:20, one launch (start us, length us, event | category | flops | bytes accessed | tf_op | source)
XLA Modules:
  0.0 117.3 jit_solution(7710222256735348513)
XLA Ops:
  0.6 0.0 copy-start
  1.4 1.3 %select_reduce_fusion = f32[2048]{0:T(1024)S(1)} fusion(f32[128]{0:T(128)} %param.10, s32[2048]{0:T(1024)} %param.9), kind=kLoop, calls=%fused_computation | loop fusion | flops 784384 | bytes 16896 | tf_op jit(solution)/shard_map/reduce_sum | solution.py:15
  2.7 1.3 %reduce-precision_convert_fusion = (bf16[128,1024]{1,0:T(8,128)(2,1)S(1)}, bf16[128]{0:T(256)(128)(2,1)S(1)}) fusion(f32[128,1024]{1,0:T(8,128)} %param.12, s32[128]{0:T(128)S(1)} %iota_add_fusion), kind=kLoop, calls=%fused_computation.5 | loop fusion | flops 786304 | bytes 787200 | tf_op jit(solution)/shard_map/convert
  4.0 0.1 broadcast_in_dim.32
  4.1 0.4 copy.10
  4.5 0.1 fusion.weights
  4.6 0.0 copy-done
  4.6 94.8 %exchange.1 = (bf16[2,2,4,256,384]{4,3,2,1,0:T(8,128)(2,1)}, bf16[2,2,2,256,384]{4,3,2,1,0:T(8,128)(2,1)S(1)}, bf16[2,4,4,32,1152]{4,3,2,1,0:T(8,128)(2,1)S(1)}) custom-call(bf16[2048,128]{1,0:T(8,128)(2,1)S(1)} %copy-done, bf16[2048,1536]{1,0:T(8,128)(2,1)} %front_cols.1, f32[2048,1]{1,0:T(8,128)S(1)} %fusion.weights, ...), custom_call_target="tpu_custom_call" | custom-call | tf_op jit(solution)/shard_map/exchange/pallas_call | solution.py:399
  99.4 17.8 %finish.1 = (f32[128,1536]{1,0:T(8,128)}, f32[768,1536]{1,0:T(8,128)}) custom-call(s32[1]{0:T(128)} %bitcast.spot, bf16[4,4,256,384]{3,2,1,0:T(8,128)(2,1)} %bitcast.9, bf16[4,2,256,384]{3,2,1,0:T(8,128)(2,1)S(1)} %bitcast.8, bf16[1024,1152]{1,0:T(8,128)(2,1)S(1)} %bitcast.7, f32[768,1536]{1,0:T(8,128)} %front.1), custom_call_target="tpu_custom_call" | custom-call | tf_op jit(solution)/shard_map/finish/pallas_call | solution.py:430
  (2 shorter events, 0.0 us)
Async XLA Ops:
  0.6 4.0 %copy-start = (bf16[2048,128]{1,0:T(8,128)(2,1)S(1)}, bf16[2048,128]{1,0:T(8,128)(2,1)}, u32[]{:S(2)}) copy-start(bf16[2048,128]{1,0:T(8,128)(2,1)} %panel.1) | copy-start | bytes 1572868
where the time goes:
time: 118 us; the launch traced here: 117 us
  Pallas kernels  113 us (96%)
  other arithmetic  2.76 us (2%)
  between operations  1.57 us (1%)
    pallas_call x1, Pallas kernels, local_kernels(): pl.pallas_call(functools.partial(exchange, ratio), out_shape=(jax.ShapeDt...  94.8 us
    pallas_call x1, Pallas kernels, local_kernels(): pl.pallas_call(finish, out_shape=(jax.ShapeDtypeStruct((slab, cols), jnp....  17.8 us

commit v1 on v0

v1 whole, which is shorter than its diff:
```python
import functools

import jax
import jax.numpy as jnp
from jax import lax
from jax.experimental import pallas as pl
from jax.experimental.pallas import tpu as pltpu
from jax.sharding import PartitionSpec as P


def live_weights(arc_ids, arc_weight, row_counts):
    row_total = arc_ids.shape[0]
    arc_total = arc_weight.shape[0]
    hit = arc_ids[:, None] == lax.broadcasted_iota(jnp.int32, (row_total, arc_total), 1)
    looked = jnp.sum(jnp.where(hit, arc_weight[None, :], 0.0), axis=1)
    is_live = lax.broadcasted_iota(jnp.int32, (row_total,), 0) < row_counts[0]
    return looked * is_live.astype(jnp.float32)


def contract_rows(left, right):
    return lax.dot_general(
        left, right, (((0,), (0,)), ((), ())), preferred_element_type=jnp.float32
    )


def local(design_panel, design_front, arc_ids, arc_weight, row_counts, panel_inverse, front):
    high = lax.reduce_precision(panel_inverse, 8, 7)
    split = jnp.concatenate([high, panel_inverse - high], axis=1).astype(jnp.bfloat16)
    inverse_whole = lax.all_gather(split, ("team", "obs"), axis=0, tiled=True)
    weights = live_weights(arc_ids, arc_weight, row_counts)
    scaled_front = (design_front.astype(jnp.float32) * weights[:, None]).astype(jnp.bfloat16)
    panel_piece = lax.all_gather(design_panel, "grid", axis=1, tiled=True)
    partial_value = contract_rows(panel_piece, scaled_front)
    slab_rows = panel_inverse.shape[0]
    place_index = lax.axis_index(("team", "obs"))
    block_part = lax.psum_scatter(partial_value, "obs", scatter_dimension=0, tiled=True)
    block_part = block_part.astype(jnp.bfloat16)
    block_whole = lax.all_gather(block_part, ("team", "obs"), axis=0, tiled=True)
    factor_cols = jnp.dot(
        inverse_whole,
        jnp.concatenate([block_whole, block_whole], axis=0),
        preferred_element_type=jnp.float32,
    )
    factor_part = lax.dynamic_slice_in_dim(factor_cols, place_index * slab_rows, slab_rows, 0)
    factor_cols = factor_cols.astype(jnp.bfloat16)
    tile_rows = front.shape[0]
    tile_ratio = factor_cols.shape[1] // tile_rows
    offset = place_index % tile_ratio * tile_rows
    own_slice = lax.dynamic_slice_in_dim(factor_cols, offset, tile_rows, 1)
    kept = jnp.where(lax.axis_index("grid") == place_index // tile_ratio, own_slice, 0)
    factor_rows = lax.psum(kept.astype(jnp.bfloat16), "grid")
    return (factor_part, front - contract_rows(factor_rows, factor_cols))


MESH = pl.DeviceIdType.MESH


def column_pieces(cols, tile_rows):
    pieces = []
    for start in range(0, cols, tile_rows):
        wide = tile_rows * 2 // 3
        pieces += [(start, wide), (start + wide, tile_rows - wide)]
    return pieces


def exchange(
    pieces, panel, front_cols, ids, arc_weight, counts, inverse_rows,
    blk, tile, inv_diag, inv_off,
    panels, scaled, weights, outgoing, from_outer, from_inner, own,
    front_sem, panel_send, panel_recv, outer_send, outer_recv, inner_send, inner_recv,
    total_send, total_recv, team_send, team_recv, tile_send, relay_send, tile_recv,
    inv_line_send, inv_line_recv, inv_grid_send, inv_grid_recv, inv_team_send, inv_team_recv,
):
    team, z, grid = lax.axis_index("team"), lax.axis_index("obs"), lax.axis_index("grid")
    rows, width = panel.shape
    lines = inv_diag.shape[1]
    share = inv_diag.shape[3]
    side = inv_off.shape[3]
    x, y = lax.rem(grid, 2), lax.div(grid, 2)
    beside_x = y * 2 + (1 - x)
    beside_y = (1 - y) * 2 + x
    across = (1 - y) * 2 + (1 - x)
    partner = 1 - team
    is_inner = (z == 1) | (z == 2)
    is_outer = jnp.logical_not(is_inner)
    mate = jnp.where(z < 2, 1 - z, 5 - z)
    other = jnp.clip(3 - z, 1, 2)
    half = lax.rem(z, 2)
    root_x = lax.div(z, 2)
    owner = y
    sends_tile = x == root_x
    root_y = team
    is_root = (x == root_x) & (y == root_y)
    at_x = (x != root_x) & (y == root_y)
    at_y = (x == root_x) & (y != root_y)
    at_across = (x != root_x) & (y != root_y)

    barrier = pltpu.get_barrier_semaphore()
    for where in (
        {"grid": beside_x}, {"grid": beside_y}, {"team": partner}, {"obs": mate},
        {"team": partner, "grid": beside_x}, {"team": partner, "grid": beside_y},
    ):
        pl.semaphore_signal(barrier, inc=1, device_id=where, device_id_type=MESH)

    @pl.when(is_inner)
    def _():
        pl.semaphore_signal(barrier, inc=1, device_id={"obs": other}, device_id_type=MESH)

    def load_front(c):
        start, wide = pieces[c]
        at = (slice(None), pl.ds(start, wide))
        return pltpu.make_async_copy(front_cols.at[at], scaled.at[at], front_sem.at[c])

    for c in range(len(pieces)):
        load_front(c).start()

    step = rows // 8
    mine = inverse_rows[pl.ds(pl.multiple_of(grid * share, share), share), :]
    high = mine.astype(jnp.bfloat16)
    row_at = lax.broadcasted_iota(jnp.int32, mine.shape, 0) + (team * side + z * width + grid * share)
    on_diagonal = lax.broadcasted_iota(jnp.int32, mine.shape, 1) == row_at
    rest = jnp.sum(jnp.where(on_diagonal, mine - high.astype(jnp.float32), 0.0), axis=1, keepdims=True)
    rest = jnp.broadcast_to(rest, (share, inv_diag.shape[4] - side)).astype(jnp.bfloat16)

    @pl.when(team == 0)
    def _():
        inv_diag[0, z, grid, :, :side] = high[:, :side]

    @pl.when(team == 1)
    def _():
        inv_diag[1, z, grid, :, :side] = high[:, side:]
        inv_off[z, grid] = high[:, :side]

    inv_diag[team, z, grid, :, side:] = rest

    pl.semaphore_wait(barrier, jnp.where(is_inner, 7, 6))

    def remote(src, dst, send, recv, where):
        return pltpu.make_async_remote_copy(
            src_ref=src, dst_ref=dst, send_sem=send, recv_sem=recv,
            device_id=where, device_id_type=MESH,
        )

    def await_on(ref, sem):
        pltpu.make_async_copy(ref, ref, sem).wait()

    panel_copies = [
        remote(panel, panels.at[0], panel_send.at[0], panel_recv.at[0], {"grid": beside_x}),
        remote(panel, panels.at[1], panel_send.at[1], panel_recv.at[1], {"grid": beside_y}),
    ]
    for copy in panel_copies:
        copy.start()
    top, bottom = pl.ds(0, rows // 2), pl.ds(rows // 2, rows // 2)
    panel_copies += [
        remote(panels.at[0, top], panels.at[2, top], panel_send.at[2], panel_recv.at[2], {"grid": beside_y}),
        remote(panels.at[1, bottom], panels.at[2, bottom], panel_send.at[3], panel_recv.at[3], {"grid": beside_x}),
    ]

    inv_parts = (
        (0, team == 0, lambda *at: inv_diag.at[(0,) + at]),
        (1, team == 1, lambda *at: inv_diag.at[(1,) + at]),
        (2, team == 1, lambda *at: inv_off.at[at]),
    )

    def inv_line(s, what):
        for k, has, of in inv_parts:
            for d, hop in ((0, 1), (1, -1)):
                held = z - hop * s
                sends = (held >= 0) & (held < lines) & (z + hop >= 0) & (z + hop < lines)
                came = z - hop * (s + 1)
                comes = (came >= 0) & (came < lines)
                if what == "start":
                    @pl.when(has & sends)
                    def _():
                        ref = of(jnp.clip(held, 0, lines - 1), grid)
                        remote(ref, ref, inv_line_send.at[k, d, s], inv_line_recv.at[k, d, s],
                               {"obs": jnp.clip(z + hop, 0, lines - 1)}).start()
                elif what == "wait":
                    @pl.when(has & comes)
                    def _():
                        await_on(of(jnp.clip(came, 0, lines - 1), grid), inv_line_recv.at[k, d, s])
                else:
                    @pl.when(has & sends)
                    def _():
                        await_on(of(jnp.clip(held, 0, lines - 1), grid), inv_line_send.at[k, d, s])

    def inv_grid(stage, what):
        every, first, last = pl.ds(0, lines), pl.ds(0, lines // 2), pl.ds(lines // 2, lines // 2)
        for k, has, of in inv_parts:
            moves = (
                (0, (every, grid), (every, beside_x), {"grid": beside_x}),
                (1, (every, grid), (every, beside_y), {"grid": beside_y}),
            ) if stage == 0 else (
                (2, (first, beside_x), (first, across), {"grid": beside_y}),
                (3, (last, beside_y), (last, across), {"grid": beside_x}),
            )

            @pl.when(has)
            def _():
                for j, sent, came, where in moves:
                    if what == "start":
                        remote(of(*sent), of(*sent), inv_grid_send.at[k, j], inv_grid_recv.at[k, j], where).start()
                    elif what == "wait":
                        await_on(of(*came), inv_grid_recv.at[k, j])
                    else:
                        await_on(of(*sent), inv_grid_send.at[k, j])

    def inv_team(what):
        for k, has, of in inv_parts:
            @pl.when(has)
            def _():
                if what == "start":
                    remote(of(), of(), inv_team_send.at[k], inv_team_recv.at[k], {"team": partner}).start()
                elif what == "drain":
                    await_on(of(), inv_team_send.at[k])

            if what == "wait":
                @pl.when(jnp.logical_not(has))
                def _():
                    await_on(of(), inv_team_recv.at[k])

    inv_line(0, "start")

    arcs = arc_weight.shape[1]
    live = counts[0]

    @pl.loop(0, rows // step)
    def _(i):
        at = pl.ds(pl.multiple_of(i * step, step), step)
        hit = ids[at, :] == lax.broadcasted_iota(jnp.int32, (step, arcs), 1)
        looked = jnp.sum(jnp.where(hit, arc_weight[...], 0.0), axis=1, keepdims=True)
        slot = lax.broadcasted_iota(jnp.int32, (step, 1), 0) + i * step
        weights[at, :] = jnp.where(slot < live, looked, 0.0)

    def scale(c):
        start, wide = pieces[c]
        load_front(c).wait()

        @pl.loop(0, rows // step)
        def _(i):
            at = pl.ds(pl.multiple_of(i * step, step), step)
            part = scaled[at, start:start + wide].astype(jnp.float32)
            scaled[at, start:start + wide] = (part * weights[at, :]).astype(jnp.bfloat16)

    count = len(pieces)
    units = [(0, c) for c in range(count)]
    units += [(r, c) for c in range(count // 2) for r in (1, 2)]
    units += [(3, c) for c in range(count // 2)]
    units += [(r, c) for c in range(count // 2, count) for r in (1, 2, 3)]
    source = (grid, beside_x, beside_y, across)

    def piece_at(c):
        return pl.ds(pieces[c][0], pieces[c][1])

    def staged(r, c):
        return pl.ds(r * width, width), piece_at(c)

    def block_rows(t, g):
        return pl.ds(pl.multiple_of((t * 4 + g) * width, width), width)

    def place(t, r, c):
        return block_rows(t, source[r]), piece_at(c)

    def tile_place(t, g, c):
        return block_rows(t, g), pl.ds(pieces[c % (count // 2)][0], pieces[c][1])

    def slot_of(r, c):
        return r * (count // 2) + c % (count // 2)

    def compute(u):
        r, c = units[u]
        if r == 0:
            scale(c)
        start, wide = pieces[c]
        left = panel[...] if r == 0 else panels[r - 1]
        total = contract_rows(left, scaled[:, start:start + wide])
        at = staged(r, c)

        @pl.when(is_inner)
        def _():
            own[at] = total

        @pl.when(is_outer)
        def _():
            outgoing[at] = total.astype(jnp.bfloat16)
            remote(outgoing.at[at], from_outer.at[at], outer_send.at[u], outer_recv.at[u], {"obs": mate}).start()

    def middle(u):
        at = staged(*units[u])
        await_on(from_outer.at[at], outer_recv.at[u])
        total = own[at] + from_outer[at].astype(jnp.float32)
        own[at] = total
        outgoing[at] = total.astype(jnp.bfloat16)
        remote(outgoing.at[at], from_inner.at[at], inner_send.at[u], inner_recv.at[u], {"obs": other}).start()

    def spread(u):
        r, c = units[u]
        ref = blk.at[place(team, r, c)]
        remote(ref, ref, team_send.at[u], team_recv.at[u], {"team": partner}).start()

        @pl.when(sends_tile & (half == c // (count // 2)))
        def _():
            k = slot_of(r, c)
            to = tile.at[tile_place(team, source[r], c)]
            remote(ref, to, tile_send.at[0, k], tile_recv.at[team, k], {"team": owner, "grid": beside_x}).start()
            remote(ref, to, tile_send.at[1, k], tile_recv.at[team, k], {"team": owner, "grid": beside_y}).start()

            @pl.when(team == owner)
            def _():
                pltpu.make_async_copy(ref, to, tile_recv.at[team, k]).start()

            @pl.when(team != owner)
            def _():
                remote(ref, to, tile_send.at[2, k], tile_recv.at[team, k], {"team": partner}).start()

    def finished_inner(u):
        r, c = units[u]
        at = staged(r, c)
        await_on(from_inner.at[at], inner_recv.at[u])
        total = own[at] + from_inner[at].astype(jnp.float32)
        spot = place(team, r, c)
        blk[spot] = total.astype(jnp.bfloat16)
        ref = blk.at[spot]
        remote(ref, ref, total_send.at[u], total_recv.at[u], {"obs": mate}).start()

    def finished_outer(u):
        r, c = units[u]
        await_on(blk.at[place(team, r, c)], total_recv.at[u])

    def tile_source(r):
        root = root_y * 2 + root_x
        flip_x = root_y * 2 + (1 - root_x)
        flip_y = (1 - root_y) * 2 + root_x
        both = (1 - root_y) * 2 + (1 - root_x)
        return (root, flip_x, flip_y, both)[r]

    def relay(u):
        r, c = units[u]
        k = slot_of(r, c)
        even = (r + c) % 2 == 0

        @pl.when((at_x if even else at_y) & (half == c // (count // 2)))
        def _():
            for t in (0, 1):
                ref = tile.at[tile_place(t, tile_source(r), c)]
                await_on(ref, tile_recv.at[t, k])
                remote(ref, ref, relay_send.at[t, k], tile_recv.at[t, k],
                       {"grid": beside_y if even else beside_x}).start()

    last = len(units)
    for i in range(last + 9):
        if i == 1:
            inv_line(0, "wait")
            inv_line(1, "start")
        if i == 2:
            inv_line(1, "wait")
            inv_line(2, "start")
        if i == 3:
            inv_line(2, "wait")
            inv_grid(0, "start")
        if i == count:
            panel_copies[0].wait_recv()
            panel_copies[2].start()
            panel_copies[1].wait_recv()
            panel_copies[3].start()
        if i == count + 2:
            inv_grid(0, "wait")
            inv_grid(1, "start")
        if i == count + count:
            panel_copies[2].wait_recv()
            panel_copies[3].wait_recv()
        if i == count + count + 2:
            inv_grid(1, "wait")
            inv_team("start")

        @pl.when(is_inner)
        def _():
            if 0 <= i - 1 < last:
                middle(i - 1)
            if 0 <= i - 3 < last:
                finished_inner(i - 3)
                spread(i - 3)

        if i < last:
            compute(i)

        @pl.when(is_outer)
        def _():
            if 0 <= i - 5 < last:
                finished_outer(i - 5)
                spread(i - 5)

        @pl.when(is_inner)
        def _():
            if 0 <= i - 5 < last:
                relay(i - 5)

        @pl.when(is_outer)
        def _():
            if 0 <= i - 8 < last:
                relay(i - 8)

    inv_team("wait")
    for u in range(last):
        r, c = units[u]
        k = slot_of(r, c)
        in_half = half == c // (count // 2)
        even = (r + c) % 2 == 0
        await_on(blk.at[place(partner, r, c)], team_recv.at[u])

        @pl.when(in_half & jnp.logical_not(at_x if even else at_y))
        def _():
            for t in (0, 1):
                await_on(tile.at[tile_place(t, tile_source(r), c)], tile_recv.at[t, k])

    for copy in panel_copies:
        copy.wait_send()
    for s in range(lines - 1):
        inv_line(s, "drain")
    inv_grid(0, "drain")
    inv_grid(1, "drain")
    inv_team("drain")
    for u in range(last):
        r, c = units[u]
        k = slot_of(r, c)
        at = staged(r, c)
        in_half = half == c // (count // 2)
        even = (r + c) % 2 == 0
        ref = blk.at[place(team, r, c)]
        await_on(ref, team_send.at[u])

        @pl.when(is_outer)
        def _():
            await_on(outgoing.at[at], outer_send.at[u])

        @pl.when(is_inner)
        def _():
            await_on(outgoing.at[at], inner_send.at[u])
            await_on(ref, total_send.at[u])

        @pl.when(in_half & sends_tile)
        def _():
            await_on(ref, tile_send.at[0, k])
            await_on(ref, tile_send.at[1, k])

            @pl.when(team != owner)
            def _():
                await_on(ref, tile_send.at[2, k])

        @pl.when(in_half & (at_x if even else at_y))
        def _():
            for t in (0, 1):
                await_on(tile.at[tile_place(t, tile_source(r), c)], relay_send.at[t, k])


def finish(blk, tile, inv_diag, inv_off, front, factor_out, front_out, cols, high, low, held, sems):
    team, z = lax.axis_index("team"), lax.axis_index("obs")
    slab, piece = factor_out.shape[0], 2 * factor_out.shape[0]
    side = inv_off.shape[0]
    whole, columns = blk.shape
    tile_cols = tile.shape[1]
    size = 2 * slab
    place = team * (side // slab) + z

    load = pltpu.make_async_copy(front, held, sems.at[0])
    load.start()

    def factor_of(source, at, r):
        rows = slice(r * size, (r + 1) * size)
        t, inner = r * size // side, r * size % side
        near = slice(inner, inner + size)
        total = inv_diag[t, near, side:side + 1].astype(jnp.float32) * source[rows, at].astype(jnp.float32)
        total += jnp.dot(
            inv_diag[t, near, :inner + size], source[t * side:t * side + inner + size, at],
            preferred_element_type=jnp.float32,
        )
        if t:
            total += jnp.dot(inv_off[near, :], source[:side, at], preferred_element_type=jnp.float32)
        return total

    for r in range(whole // size):
        rows = slice(r * size, (r + 1) * size)
        for start in range(0, columns, piece):
            at = slice(start, start + piece)
            value = factor_of(blk, at, r)
            cols[rows, at] = value.astype(jnp.bfloat16)
            for part in range(size // slab):
                @pl.when(place == r * (size // slab) + part)
                def _():
                    factor_out[:, at] = value[part * slab:(part + 1) * slab]
        for start in range(0, tile_cols, piece):
            at = slice(start, start + piece)
            value = factor_of(tile, at, r).T
            upper = value.astype(jnp.bfloat16)
            high[at, rows] = upper
            low[at, rows] = (value - upper.astype(jnp.float32)).astype(jnp.bfloat16)

    load.wait()
    stores = []
    for top in range(0, tile_cols, piece):
        for start in range(0, columns, 2 * piece):
            near, at = slice(top, top + piece), slice(start, start + 2 * piece)
            update = jnp.dot(high[near, :], cols[:, at], preferred_element_type=jnp.float32)
            update += jnp.dot(low[near, :], cols[:, at], preferred_element_type=jnp.float32)
            held[near, at] = held[near, at] - update
            spot = (pl.ds(top, piece), pl.ds(start, 2 * piece))
            stores.append(
                pltpu.make_async_copy(held.at[spot], front_out.at[spot], sems.at[1 + len(stores)])
            )
            stores[-1].start()
    for store in stores:
        store.wait()


def local_kernels(lines, grids, design_panel, design_front, arc_ids, arc_weight, row_counts, panel_inverse, front):
    bf16 = jnp.bfloat16
    slab, whole = panel_inverse.shape
    rows, width = design_panel.shape
    cols = design_front.shape[1]
    tile_rows = front.shape[0]
    side = whole // 2
    share = slab // grids
    pieces = column_pieces(cols, tile_rows)
    vmem = pl.BlockSpec(memory_space=pltpu.VMEM)
    smem = pl.BlockSpec(memory_space=pltpu.SMEM)
    hbm = pl.BlockSpec(memory_space=pl.ANY)
    dma = pltpu.SemaphoreType.DMA
    hops = lines - 1
    units = grids * len(pieces)
    slots = units // 2
    blk, tile, inv_diag, inv_off = pl.pallas_call(
        functools.partial(exchange, pieces),
        out_shape=(
            jax.ShapeDtypeStruct((whole, cols), bf16),
            jax.ShapeDtypeStruct((whole, tile_rows), bf16),
            jax.ShapeDtypeStruct((2, lines, grids, share, side + 128), bf16),
            jax.ShapeDtypeStruct((lines, grids, share, side), bf16),
        ),
        in_specs=[vmem, hbm, vmem, vmem, smem, vmem],
        out_specs=(vmem,) * 4,
        scratch_shapes=[
            pltpu.VMEM((grids - 1, rows, width), bf16),
            pltpu.VMEM((rows, cols), bf16),
            pltpu.VMEM((rows, 1), jnp.float32),
            pltpu.VMEM((grids * width, cols), bf16),
            pltpu.VMEM((grids * width, cols), bf16),
            pltpu.VMEM((grids * width, cols), bf16),
            pltpu.VMEM((grids * width, cols), jnp.float32),
            dma((len(pieces),)), dma((4,)), dma((4,)),
            dma((units,)), dma((units,)), dma((units,)), dma((units,)),
            dma((units,)), dma((units,)), dma((units,)), dma((units,)),
            dma((3, slots)), dma((2, slots)), dma((2, slots)),
            dma((3, 2, hops)), dma((3, 2, hops)), dma((3, 4)), dma((3, 4)), dma((3,)), dma((3,)),
        ],
        compiler_params=pltpu.CompilerParams(
            collective_id=0, has_side_effects=True, vmem_limit_bytes=48 * 2**20
        ),
        name="exchange",
    )(design_panel, design_front, arc_ids[:, None], arc_weight[None, :], row_counts, panel_inverse)
    inv_diag = inv_diag.reshape((2, side, side + 128))
    inv_off = inv_off.reshape((side, side))
    return pl.pallas_call(
        finish,
        out_shape=(
            jax.ShapeDtypeStruct((slab, cols), jnp.float32),
            jax.ShapeDtypeStruct(front.shape, jnp.float32),
        ),
        in_specs=[vmem] * 4 + [hbm],
        out_specs=(vmem, hbm),
        scratch_shapes=[
            pltpu.VMEM((whole, cols), bf16),
            pltpu.VMEM((tile_rows, whole), bf16),
            pltpu.VMEM((tile_rows, whole), bf16),
            pltpu.VMEM(front.shape, jnp.float32),
            dma((1 + tile_rows * cols // (8 * slab * slab),)),
        ],
        compiler_params=pltpu.CompilerParams(vmem_limit_bytes=48 * 2**20),
        name="finish",
    )(blk, tile, inv_diag, inv_off, front)


def solution(mesh):
    placed = (
        P("obs", ("team", "grid")),
        P("obs", "grid"),
        P("obs"),
        P(),
        P("obs"),
        P(("team", "obs"), None),
        P(("team", "obs"), "grid"),
    )
    sizes = mesh.shape
    fits = sizes["team"] == 2 and sizes["obs"] == 4 and sizes["grid"] == 4
    return jax.shard_map(
        functools.partial(local_kernels, sizes["obs"], sizes["grid"]) if fits else local,
        mesh=mesh,
        in_specs=placed,
        out_specs=(P(("team", "obs"), "grid"), P(("team", "obs"), "grid")),
        check_vma=False,
    )
```

time: 118 us -> 96 us (0.81)
  the two profiles are of different devices: /device:TPU:20 before, /device:TPU:25 now
where the time goes in v1:
time: 96 us; the launch traced here: 95.7 us
  Pallas kernels  90.4 us (94%)
  local copies, waits for them, and re-layouts  3.79 us (4%)
  between operations  1.46 us (2%)
    pallas_call x1, Pallas kernels, local_kernels(): pl.pallas_call(functools.partial(exchange, pieces), out_shape=(jax.ShapeD...  72.3 us
    pallas_call x1, Pallas kernels, local_kernels(): pl.pallas_call(finish, out_shape=(jax.ShapeDtypeStruct((slab, cols), jnp....  18.2 us
    unnamed x6, local copies, waits for them, and re-layouts  2.74 us

profile of v1, /device:TPU:25, one launch (start us, length us, event | category | flops | bytes accessed | tf_op | source)
XLA Modules:
  0.0 95.7 jit_solution(4588763142350109177)
XLA Ops:
  1.3 1.1 %copy.9.ids = s32[2048,1]{1,0:T(8,128)S(1)} copy(s32[2048,1]{0,1:T(1,128)} %bitcast.7) | data formatting | bytes 16384 | tf_op jit(solution)/shard_map/broadcast_in_dim | solution.py:559
  2.3 0.0 copy-start
  2.4 1.0 %copy-done = bf16[2048,128]{1,0:T(8,128)(2,1)S(1)} copy-done((bf16[2048,128]{1,0:T(8,128)(2,1)S(1)}, bf16[2048,128]{1,0:T(8,128)(2,1)}, u32[]{:S(2)}) %copy-start) | copy-done | bytes 524312
  3.4 0.0 copy-start.1
  3.4 1.0 %copy-done.1 = f32[128,1024]{1,0:T(8,128)S(1)} copy-done((f32[128,1024]{1,0:T(8,128)S(1)}, f32[128,1024]{1,0:T(8,128)}, u32[]{:S(2)}) %copy-start.1) | copy-done | bytes 524312
  4.4 0.0 copy-start.2
  4.4 0.7 copy-done.2
  5.1 72.3 %exchange.1 = (bf16[1024,1536]{1,0:T(8,128)(2,1)}, bf16[1024,768]{1,0:T(8,128)(2,1)S(1)}, bf16[2,4,4,32,640]{4,3,2,1,0:T(8,128)(2,1)S(1)}, bf16[4,4,32,512]{3,2,1,0:T(8,128)(2,1)S(1)}) custom-call(bf16[2048,128]{1,0:T(8,128)(2,1)S(1)} %copy-done, bf16[2048,1536]{1,0:T(8,128)(2,1)} %front_cols.1, s32[2048,1]{1,0:T(8,128)S(1)} %copy.9.ids, ...), custom_call_target="tpu_custom_call" | custom-call | tf_op jit(solution)/shard_map/exchange/pallas_call | solution.py:531
  77.3 18.2 %finish.1 = (f32[128,1536]{1,0:T(8,128)}, f32[768,1536]{1,0:T(8,128)}) custom-call(bf16[1024,1536]{1,0:T(8,128)(2,1)} %get-tuple-element.6.blk, bf16[1024,768]{1,0:T(8,128)(2,1)S(1)} %get-tuple-element.7.tile, bf16[2,512,640]{2,1,0:T(8,128)(2,1)S(1)} %bitcast.4, bf16[512,512]{1,0:T(8,128)(2,1)S(1)} %bitcast.5, f32[768,1536]{1,0:T(8,128)} %front.1), custom_call_target="tpu_custom_call" | custom-call | tf_op jit(solution)/shard_map/finish/pallas_call | solution.py:562
Async XLA Ops:
  2.3 1.0 %copy-start = (bf16[2048,128]{1,0:T(8,128)(2,1)S(1)}, bf16[2048,128]{1,0:T(8,128)(2,1)}, u32[]{:S(2)}) copy-start(bf16[2048,128]{1,0:T(8,128)(2,1)} %panel.1) | copy-start | bytes 1572868
  3.4 1.0 %copy-start.1 = (f32[128,1024]{1,0:T(8,128)S(1)}, f32[128,1024]{1,0:T(8,128)}, u32[]{:S(2)}) copy-start(f32[128,1024]{1,0:T(8,128)} %inverse_rows.1) | copy-start | bytes 1572868
  4.4 0.7 copy-start.2

commit v2 on v1

--- a/solution.py
+++ b/solution.py
@@ -64,10 +64,11 @@
 
 
 def exchange(
-    pieces, panel, front_cols, ids, arc_weight, counts, inverse_rows,
-    blk, tile, inv_diag, inv_off,
+    pieces, panel, front_cols, ids_hbm, arc_hbm, counts, inverse_hbm, front,
+    cols, high, low, held, factor_part,
+    blk, tile, inv_diag, inv_off, ids, arc_weight, inverse_rows,
     panels, scaled, weights, outgoing, from_outer, from_inner, own,
-    front_sem, panel_send, panel_recv, outer_send, outer_recv, inner_send, inner_recv,
+    front_sem, local_sem, panel_send, panel_recv, outer_send, outer_recv, inner_send, inner_recv,
     total_send, total_recv, team_send, team_recv, tile_send, relay_send, tile_recv,
     inv_line_send, inv_line_recv, inv_grid_send, inv_grid_recv, inv_team_send, inv_team_recv,
 ):
@@ -111,25 +112,40 @@
         at = (slice(None), pl.ds(start, wide))
         return pltpu.make_async_copy(front_cols.at[at], scaled.at[at], front_sem.at[c])
 
-    for c in range(len(pieces)):
+    count = len(pieces)
+    load_inverse = pltpu.make_async_copy(inverse_hbm, inverse_rows, local_sem.at[0])
+    load_ids = pltpu.make_async_copy(ids_hbm, ids, local_sem.at[1])
+    load_arcs = pltpu.make_async_copy(arc_hbm, arc_weight, local_sem.at[2])
+    load_panel = pltpu.make_async_copy(panel, panels.at[0], local_sem.at[3])
+    load_held = pltpu.make_async_copy(front, held, local_sem.at[4])
+    load_inverse.start()
+    load_ids.start()
+    load_arcs.start()
+    load_front(0).start()
+    load_panel.start()
+    for c in range(count // 2, count):
         load_front(c).start()
+    for c in range(1, count // 2):
+        load_front(c).start()
+    load_held.start()
 
     step = rows // 8
+    load_inverse.wait()
     mine = inverse_rows[pl.ds(pl.multiple_of(grid * share, share), share), :]
-    high = mine.astype(jnp.bfloat16)
+    rounded = mine.astype(jnp.bfloat16)
     row_at = lax.broadcasted_iota(jnp.int32, mine.shape, 0) + (team * side + z * width + grid * share)
     on_diagonal = lax.broadcasted_iota(jnp.int32, mine.shape, 1) == row_at
-    rest = jnp.sum(jnp.where(on_diagonal, mine - high.astype(jnp.float32), 0.0), axis=1, keepdims=True)
+    rest = jnp.sum(jnp.where(on_diagonal, mine - rounded.astype(jnp.float32), 0.0), axis=1, keepdims=True)
     rest = jnp.broadcast_to(rest, (share, inv_diag.shape[4] - side)).astype(jnp.bfloat16)
 
     @pl.when(team == 0)
     def _():
-        inv_diag[0, z, grid, :, :side] = high[:, :side]
+        inv_diag[0, z, grid, :, :side] = rounded[:, :side]
 
     @pl.when(team == 1)
     def _():
-        inv_diag[1, z, grid, :, :side] = high[:, side:]
-        inv_off[z, grid] = high[:, :side]
+        inv_diag[1, z, grid, :, :side] = rounded[:, side:]
+        inv_off[z, grid] = rounded[:, :side]
 
     inv_diag[team, z, grid, :, side:] = rest
 
@@ -145,15 +161,15 @@
         pltpu.make_async_copy(ref, ref, sem).wait()
 
     panel_copies = [
-        remote(panel, panels.at[0], panel_send.at[0], panel_recv.at[0], {"grid": beside_x}),
-        remote(panel, panels.at[1], panel_send.at[1], panel_recv.at[1], {"grid": beside_y}),
+        remote(panel, panels.at[1], panel_send.at[0], panel_recv.at[0], {"grid": beside_x}),
+        remote(panel, panels.at[2], panel_send.at[1], panel_recv.at[1], {"grid": beside_y}),
     ]
     for copy in panel_copies:
         copy.start()
     top, bottom = pl.ds(0, rows // 2), pl.ds(rows // 2, rows // 2)
     panel_copies += [
-        remote(panels.at[0, top], panels.at[2, top], panel_send.at[2], panel_recv.at[2], {"grid": beside_y}),
-        remote(panels.at[1, bottom], panels.at[2, bottom], panel_send.at[3], panel_recv.at[3], {"grid": beside_x}),
+        remote(panels.at[1, top], panels.at[3, top], panel_send.at[2], panel_recv.at[2], {"grid": beside_y}),
+        remote(panels.at[2, bottom], panels.at[3, bottom], panel_send.at[3], panel_recv.at[3], {"grid": beside_x}),
     ]
 
     inv_parts = (
@@ -223,14 +239,20 @@
 
     arcs = arc_weight.shape[1]
     live = counts[0]
-
-    @pl.loop(0, rows // step)
-    def _(i):
-        at = pl.ds(pl.multiple_of(i * step, step), step)
-        hit = ids[at, :] == lax.broadcasted_iota(jnp.int32, (step, arcs), 1)
-        looked = jnp.sum(jnp.where(hit, arc_weight[...], 0.0), axis=1, keepdims=True)
-        slot = lax.broadcasted_iota(jnp.int32, (step, 1), 0) + i * step
-        weights[at, :] = jnp.where(slot < live, looked, 0.0)
+    load_ids.wait()
+    load_arcs.wait()
+    lane = lax.broadcasted_iota(jnp.int32, (arcs, arcs), 1)
+    place_of = lax.broadcasted_iota(jnp.int32, (arcs, arcs), 0)
+
+    def upright(line):
+        return jnp.sum(jnp.where(lane == place_of, line, 0), axis=1, keepdims=True)
+
+    arc_column = upright(arc_weight[...])
+    for i in range(rows // arcs):
+        hit = ids[i:i + 1, :] == place_of
+        looked = jnp.sum(jnp.where(hit, arc_column, 0.0), axis=0, keepdims=True)
+        slot = lax.broadcasted_iota(jnp.int32, (1, arcs), 1) + i * arcs
+        weights[i * arcs:(i + 1) * arcs, :] = upright(jnp.where(slot < live, looked, 0.0))
 
     def scale(c):
         start, wide = pieces[c]
@@ -242,11 +264,9 @@
             part = scaled[at, start:start + wide].astype(jnp.float32)
             scaled[at, start:start + wide] = (part * weights[at, :]).astype(jnp.bfloat16)
 
-    count = len(pieces)
-    units = [(0, c) for c in range(count)]
-    units += [(r, c) for c in range(count // 2) for r in (1, 2)]
-    units += [(3, c) for c in range(count // 2)]
-    units += [(r, c) for c in range(count // 2, count) for r in (1, 2, 3)]
+    units = [(0, 0), (0, count // 2)]
+    units += [(r, 0) for r in (1, 2, 3)] + [(r, count // 2) for r in (1, 2, 3)]
+    units += [(r, c) for k in range(1, count // 2) for c in (k, k + count // 2) for r in (0, 1, 2, 3)]
     source = (grid, beside_x, beside_y, across)
 
     def piece_at(c):
@@ -272,8 +292,7 @@
         if r == 0:
             scale(c)
         start, wide = pieces[c]
-        left = panel[...] if r == 0 else panels[r - 1]
-        total = contract_rows(left, scaled[:, start:start + wide])
+        total = contract_rows(panels[r], scaled[:, start:start + wide])
         at = staged(r, c)
 
         @pl.when(is_inner)
@@ -347,8 +366,85 @@
                 remote(ref, ref, relay_send.at[t, k], tile_recv.at[t, k],
                        {"grid": beside_y if even else beside_x}).start()
 
+    whole, columns = blk.shape
+    slab = inverse_rows.shape[0]
+    size = 2 * slab
+    blocks = whole // size
+    pair = team * lines + z
+
+    def factor_of(ref, at, r):
+        t, inner = r * size // side, r * size % side
+        first, near = inner // slab, slice(r * size, (r + 1) * size)
+        ahead = inv_diag[t, first:first + 2].reshape((size, inv_diag.shape[4]))
+        total = ahead[:, side:side + 1].astype(jnp.float32) * ref[near, at].astype(jnp.float32)
+        total += jnp.dot(
+            ahead[:, :inner + size], ref[t * side:t * side + inner + size, at],
+            preferred_element_type=jnp.float32,
+        )
+        if t:
+            behind = inv_off[first:first + 2].reshape((size, side))
+            total += jnp.dot(behind, ref[:side, at], preferred_element_type=jnp.float32)
+        return total
+
+    def await_columns(c):
+        for u in range(last):
+            if units[u][1] == c:
+                await_on(blk.at[place(partner, *units[u])], team_recv.at[u])
+
+    def factor_columns(c, r):
+        at = slice(pieces[c][0], pieces[c][0] + pieces[c][1])
+        value = factor_of(blk, at, r)
+        cols[r * size:(r + 1) * size, at] = value.astype(jnp.bfloat16)
+        for part in range(size // slab):
+            @pl.when(pair == r * (size // slab) + part)
+            def _():
+                factor_part[:, at] = value[part * slab:(part + 1) * slab]
+
+    def await_tile(c):
+        for u in range(last):
+            r, d = units[u]
+            if d % (count // 2) == c:
+                k = slot_of(r, d)
+                even = (r + d) % 2 == 0
+
+                @pl.when((half == d // (count // 2)) & jnp.logical_not(at_x if even else at_y))
+                def _():
+                    for t in (0, 1):
+                        await_on(tile.at[tile_place(t, tile_source(r), d)], tile_recv.at[t, k])
+
+    def factor_tile(c, r):
+        at = slice(pieces[c][0], pieces[c][0] + pieces[c][1])
+        value = factor_of(tile, at, r)
+        upper = value.astype(jnp.bfloat16)
+        high[r * size:(r + 1) * size, at] = upper
+        low[r * size:(r + 1) * size, at] = (value - upper.astype(jnp.float32)).astype(jnp.bfloat16)
+
+    def update(c, part):
+        at = slice(pieces[c][0], pieces[c][0] + pieces[c][1])
+        near = slice(part * size, (part + 1) * size)
+        change = contract_rows(high[:, near], cols[:, at]) + contract_rows(low[:, near], cols[:, at])
+        held[near, at] = held[near, at] - change
+
     last = len(units)
-    for i in range(last + 9):
+    far = count // 2
+    tasks = {
+        10: [lambda: inv_team("wait"), lambda: await_columns(0)] + [lambda r=r: factor_columns(0, r) for r in range(blocks - 1)],
+        11: [lambda: factor_columns(0, blocks - 1)],
+        13: [lambda: await_columns(far)] + [lambda r=r: factor_columns(far, r) for r in range(blocks - 1)],
+        14: [lambda: factor_columns(far, blocks - 1)],
+        17: [lambda: await_columns(1)] + [lambda r=r: factor_columns(1, r) for r in range(blocks)],
+        18: [lambda: await_tile(0)] + [lambda r=r: factor_tile(0, r) for r in range(blocks - 1)],
+        19: [lambda: factor_tile(0, blocks - 1), load_held.wait],
+        20: [lambda: update(0, 0)],
+        21: [lambda: update(0, 1)],
+        22: [lambda: update(far, 0)],
+        23: [lambda: update(far, 1), lambda: update(1, 0), lambda: update(1, 1)],
+        24: [lambda: await_columns(far + 1)] + [lambda r=r: factor_columns(far + 1, r) for r in range(blocks)],
+        25: [lambda: await_tile(1)] + [lambda r=r: factor_tile(1, r) for r in range(blocks)],
+    }
+    for i in range(last + 10):
+        if i == 0:
+            load_panel.wait()
         if i == 1:
             inv_line(0, "wait")
             inv_line(1, "start")
@@ -358,18 +454,10 @@
         if i == 3:
             inv_line(2, "wait")
             inv_grid(0, "start")
-        if i == count:
-            panel_copies[0].wait_recv()
-            panel_copies[2].start()
-            panel_copies[1].wait_recv()
-            panel_copies[3].start()
-        if i == count + 2:
+        if i == 6:
             inv_grid(0, "wait")
             inv_grid(1, "start")
-        if i == count + count:
-            panel_copies[2].wait_recv()
-            panel_copies[3].wait_recv()
-        if i == count + count + 2:
+        if i == 8:
             inv_grid(1, "wait")
             inv_team("start")
 
@@ -381,6 +469,15 @@
                 finished_inner(i - 3)
                 spread(i - 3)
 
+        if i == 2:
+            panel_copies[0].wait_recv()
+            panel_copies[2].start()
+            panel_copies[1].wait_recv()
+            panel_copies[3].start()
+        if i == 4:
+            panel_copies[2].wait_recv()
+            panel_copies[3].wait_recv()
+
         if i < last:
             compute(i)
 
@@ -397,21 +494,11 @@
 
         @pl.when(is_outer)
         def _():
-            if 0 <= i - 8 < last:
-                relay(i - 8)
-
-    inv_team("wait")
-    for u in range(last):
-        r, c = units[u]
-        k = slot_of(r, c)
-        in_half = half == c // (count // 2)
-        even = (r + c) % 2 == 0
-        await_on(blk.at[place(partner, r, c)], team_recv.at[u])
-
-        @pl.when(in_half & jnp.logical_not(at_x if even else at_y))
-        def _():
-            for t in (0, 1):
-                await_on(tile.at[tile_place(t, tile_source(r), c)], tile_recv.at[t, k])
+            if 0 <= i - 7 < last:
+                relay(i - 7)
+
+        for task in tasks.get(i, ()):
+            task()
 
     for copy in panel_copies:
         copy.wait_send()
@@ -453,63 +540,34 @@
                 await_on(tile.at[tile_place(t, tile_source(r), c)], relay_send.at[t, k])
 
 
-def finish(blk, tile, inv_diag, inv_off, front, factor_out, front_out, cols, high, low, held, sems):
-    team, z = lax.axis_index("team"), lax.axis_index("obs")
-    slab, piece = factor_out.shape[0], 2 * factor_out.shape[0]
-    side = inv_off.shape[0]
-    whole, columns = blk.shape
-    tile_cols = tile.shape[1]
-    size = 2 * slab
-    place = team * (side // slab) + z
-
-    load = pltpu.make_async_copy(front, held, sems.at[0])
-    load.start()
-
-    def factor_of(source, at, r):
-        rows = slice(r * size, (r + 1) * size)
-        t, inner = r * size // side, r * size % side
-        near = slice(inner, inner + size)
-        total = inv_diag[t, near, side:side + 1].astype(jnp.float32) * source[rows, at].astype(jnp.float32)
-        total += jnp.dot(
-            inv_diag[t, near, :inner + size], source[t * side:t * side + inner + size, at],
-            preferred_element_type=jnp.float32,
-        )
-        if t:
-            total += jnp.dot(inv_off[near, :], source[:side, at], preferred_element_type=jnp.float32)
-        return total
-
-    for r in range(whole // size):
-        rows = slice(r * size, (r + 1) * size)
-        for start in range(0, columns, piece):
-            at = slice(start, start + piece)
-            value = factor_of(blk, at, r)
-            cols[rows, at] = value.astype(jnp.bfloat16)
-            for part in range(size // slab):
-                @pl.when(place == r * (size // slab) + part)
-                def _():
-                    factor_out[:, at] = value[part * slab:(part + 1) * slab]
-        for start in range(0, tile_cols, piece):
-            at = slice(start, start + piece)
-            value = factor_of(tile, at, r).T
-            upper = value.astype(jnp.bfloat16)
-            high[at, rows] = upper
-            low[at, rows] = (value - upper.astype(jnp.float32)).astype(jnp.bfloat16)
-
-    load.wait()
-    stores = []
-    for top in range(0, tile_cols, piece):
-        for start in range(0, columns, 2 * piece):
-            near, at = slice(top, top + piece), slice(start, start + 2 * piece)
-            update = jnp.dot(high[near, :], cols[:, at], preferred_element_type=jnp.float32)
-            update += jnp.dot(low[near, :], cols[:, at], preferred_element_type=jnp.float32)
-            held[near, at] = held[near, at] - update
-            spot = (pl.ds(top, piece), pl.ds(start, 2 * piece))
-            stores.append(
-                pltpu.make_async_copy(held.at[spot], front_out.at[spot], sems.at[1 + len(stores)])
-            )
-            stores[-1].start()
-    for store in stores:
-        store.wait()
+def finish(pieces, cols, high, low, held, factor_part, factor_out, front_out, done, sems):
+    count = len(pieces)
+    tile_rows, columns = held.shape
+    wide = pieces[0][1]
+    ready = [0, count // 2, 1]
+    copies = [pltpu.make_async_copy(factor_part, factor_out, sems.at[0])]
+
+    def store(ref, near, start, width):
+        at = (pl.ds(near[0], near[1]), pl.ds(start, width))
+        copies.append(pltpu.make_async_copy(ref.at[at], front_out.at[at], sems.at[len(copies)]))
+        copies[-1].start()
+
+    copies[0].start()
+    for c in ready:
+        store(held, (0, wide), *pieces[c])
+
+    def update(near, start, width):
+        rows, at = slice(near[0], near[0] + near[1]), slice(start, start + width)
+        change = contract_rows(high[:, rows], cols[:, at]) + contract_rows(low[:, rows], cols[:, at])
+        done[rows, at] = held[rows, at] - change
+        store(done, near, start, width)
+
+    final = pieces[count // 2 + 1]
+    update((0, wide), *final)
+    for start, width in pieces[0::2] + pieces[1::2]:
+        update((wide, tile_rows - wide), start, width)
+    for copy in copies:
+        copy.wait()
 
 
 def local_kernels(lines, grids, design_panel, design_front, arc_ids, arc_weight, row_counts, panel_inverse, front):
@@ -523,60 +581,70 @@
     pieces = column_pieces(cols, tile_rows)
     vmem = pl.BlockSpec(memory_space=pltpu.VMEM)
     smem = pl.BlockSpec(memory_space=pltpu.SMEM)
-    hbm = pl.BlockSpec(memory_space=pl.ANY)
+    hbm = pl.BlockSpec(memory_space=pltpu.HBM)
     dma = pltpu.SemaphoreType.DMA
     hops = lines - 1
+    arcs = arc_weight.shape[0]
+
+    def stay(value):
+        return pltpu.with_memory_space_constraint(value, pltpu.HBM)
+
     units = grids * len(pieces)
     slots = units // 2
-    blk, tile, inv_diag, inv_off = pl.pallas_call(
+    f32 = jnp.float32
+    outs = pl.pallas_call(
         functools.partial(exchange, pieces),
         out_shape=(
             jax.ShapeDtypeStruct((whole, cols), bf16),
             jax.ShapeDtypeStruct((whole, tile_rows), bf16),
-            jax.ShapeDtypeStruct((2, lines, grids, share, side + 128), bf16),
-            jax.ShapeDtypeStruct((lines, grids, share, side), bf16),
+            jax.ShapeDtypeStruct((whole, tile_rows), bf16),
+            jax.ShapeDtypeStruct(front.shape, f32),
+            jax.ShapeDtypeStruct((slab, cols), f32),
         ),
-        in_specs=[vmem, hbm, vmem, vmem, smem, vmem],
-        out_specs=(vmem,) * 4,
+        in_specs=[hbm, hbm, hbm, hbm, smem, hbm, hbm],
+        out_specs=(vmem,) * 5,
         scratch_shapes=[
-            pltpu.VMEM((grids - 1, rows, width), bf16),
+            pltpu.VMEM((whole, cols), bf16),
+            pltpu.VMEM((whole, tile_rows), bf16),
+            pltpu.VMEM((2, lines, grids, share, side + 128), bf16),
+            pltpu.VMEM((lines, grids, share, side), bf16),
+            pltpu.VMEM((rows // arcs, arcs), jnp.int32),
+            pltpu.VMEM((1, arcs), f32),
+            pltpu.VMEM((slab, whole), f32),
+            pltpu.VMEM((grids, rows, width), bf16),
             pltpu.VMEM((rows, cols), bf16),
-            pltpu.VMEM((rows, 1), jnp.float32),
+            pltpu.VMEM((rows, 1), f32),
             pltpu.VMEM((grids * width, cols), bf16),
             pltpu.VMEM((grids * width, cols), bf16),
             pltpu.VMEM((grids * width, cols), bf16),
-            pltpu.VMEM((grids * width, cols), jnp.float32),
-            dma((len(pieces),)), dma((4,)), dma((4,)),
+            pltpu.VMEM((grids * width, cols), f32),
+            dma((len(pieces),)), dma((5,)), dma((4,)), dma((4,)),
             dma((units,)), dma((units,)), dma((units,)), dma((units,)),
             dma((units,)), dma((units,)), dma((units,)), dma((units,)),
             dma((3, slots)), dma((2, slots)), dma((2, slots)),
             dma((3, 2, hops)), dma((3, 2, hops)), dma((3, 4)), dma((3, 4)), dma((3,)), dma((3,)),
         ],
         compiler_params=pltpu.CompilerParams(
-            collective_id=0, has_side_effects=True, vmem_limit_bytes=48 * 2**20
+            collective_id=0, has_side_effects=True, vmem_limit_bytes=30 * 2**20
         ),
         name="exchange",
-    )(design_panel, design_front, arc_ids[:, None], arc_weight[None, :], row_counts, panel_inverse)
-    inv_diag = inv_diag.reshape((2, side, side + 128))
-    inv_off = inv_off.reshape((side, side))
+    )(stay(design_panel), stay(design_front), stay(arc_ids.reshape((rows // arcs, arcs))),
+      stay(arc_weight[None, :]), row_counts, stay(panel_inverse), stay(front))
     return pl.pallas_call(
-        finish,
+        functools.partial(finish, pieces),
         out_shape=(
-            jax.ShapeDtypeStruct((slab, cols), jnp.float32),
-            jax.ShapeDtypeStruct(front.shape, jnp.float32),
+            jax.ShapeDtypeStruct((slab, cols), f32),
+            jax.ShapeDtypeStruct(front.shape, f32),
         ),
-        in_specs=[vmem] * 4 + [hbm],
-        out_specs=(vmem, hbm),
+        in_specs=[vmem] * 5,
+        out_specs=(hbm, hbm),
         scratch_shapes=[
-            pltpu.VMEM((whole, cols), bf16),
-            pltpu.VMEM((tile_rows, whole), bf16),
-            pltpu.VMEM((tile_rows, whole), bf16),
-            pltpu.VMEM(front.shape, jnp.float32),
-            dma((1 + tile_rows * cols // (8 * slab * slab),)),
+            pltpu.VMEM(front.shape, f32),
+            dma((2 * len(pieces) + 1,)),
         ],
-        compiler_params=pltpu.CompilerParams(vmem_limit_bytes=48 * 2**20),
+        compiler_params=pltpu.CompilerParams(vmem_limit_bytes=12 * 2**20),
         name="finish",
-    )(blk, tile, inv_diag, inv_off, front)
+    )(*outs)
 
 
 def solution(mesh):

time: 96 us -> 77.6 us (0.81)
  the two profiles are of different devices: /device:TPU:25 before, /device:TPU:0 now
where the time goes in v2:
time: 77.6 us; the launch traced here: 77.4 us
  Pallas kernels  76 us (98%)
  between operations  1.45 us (2%)
    pallas_call x1, Pallas kernels, local_kernels(): pl.pallas_call(functools.partial(exchange, pieces), out_shape=(jax.ShapeD...  72.7 us
    pallas_call x1, Pallas kernels, local_kernels(): pl.pallas_call(functools.partial(finish, pieces), out_shape=(jax.ShapeDty...  3.28 us

profile of v2, /device:TPU:0, one launch (start us, length us, event | category | flops | bytes accessed | tf_op | source)
XLA Modules:
  0.0 77.4 jit_solution(9108346710333989942)
XLA Ops:
  1.3 72.7 %exchange.1 = (bf16[1024,1536]{1,0:T(8,128)(2,1)S(1)}, bf16[1024,768]{1,0:T(8,128)(2,1)S(1)}, bf16[1024,768]{1,0:T(8,128)(2,1)S(1)}, f32[768,1536]{1,0:T(8,128)S(1)}, f32[128,1536]{1,0:T(8,128)S(1)}) custom-call(bf16[2048,128]{1,0:T(8,128)(2,1)} %panel.1, bf16[2048,1536]{1,0:T(8,128)(2,1)} %front_cols.1, s32[16,128]{1,0:T(8,128)} %bitcast.2, ...), custom_call_target="tpu_custom_call" | custom-call | tf_op jit(solution)/shard_map/exchange/pallas_call | solution.py:595
  74.0 3.3 %finish.1 = (f32[128,1536]{1,0:T(8,128)}, f32[768,1536]{1,0:T(8,128)}) custom-call(bf16[1024,1536]{1,0:T(8,128)(2,1)S(1)} %get-tuple-element.7.cols, bf16[1024,768]{1,0:T(8,128)(2,1)S(1)} %get-tuple-element.8.high, bf16[1024,768]{1,0:T(8,128)(2,1)S(1)} %get-tuple-element.9.low, f32[768,1536]{1,0:T(8,128)S(1)} %get-tuple-element.10.held, ...), custom_call_target="tpu_custom_call" | custom-call | tf_op jit(solution)/shard_map/finish/pallas_call | solution.py:633

commit v3 on v2

--- a/solution.py
+++ b/solution.py
@@ -55,16 +55,33 @@
 MESH = pl.DeviceIdType.MESH
 
 
-def column_pieces(cols, tile_rows):
-    pieces = []
-    for start in range(0, cols, tile_rows):
-        wide = tile_rows * 2 // 3
-        pieces += [(start, wide), (start + wide, tile_rows - wide)]
-    return pieces
+UNITS = (
+    (0, 0), (0, 3), (0, 1), (0, 4), (0, 2), (0, 5), (1, 0), (1, 3), (1, 1), (1, 4), (2, 0), (2, 3), (2, 1),
+    (2, 4), (3, 0), (3, 3), (3, 1), (3, 4), (1, 2), (2, 2), (3, 2), (1, 5), (2, 5), (3, 5)
+)
+INNER = (
+    (0, 0, 4), (0, 1, 6), (0, 2, 7), (1, 0, 8), (0, 3, 8), (0, 4, 10), (1, 1, 10), (0, 5, 10), (1, 2, 10), (0,
+    6, 10), (1, 3, 11), (0, 7, 12), (1, 4, 12), (0, 8, 14), (1, 5, 14), (0, 9, 14), (1, 6, 14), (0, 10, 14),
+    (1, 7, 14), (0, 11, 14), (1, 8, 15), (0, 12, 16), (1, 9, 16), (0, 13, 18), (1, 10, 18), (0, 14, 19), (2,
+    0, 19), (1, 11, 19), (2, 1, 19), (0, 15, 21), (1, 12, 21), (2, 2, 21), (2, 3, 21), (0, 16, 22), (1, 13,
+    22), (2, 4, 22), (2, 5, 22), (0, 17, 23), (2, 6, 23), (1, 14, 23), (2, 7, 23), (2, 8, 24), (0, 18, 24),
+    (1, 15, 24), (2, 9, 24), (0, 19, 28), (1, 16, 28), (2, 10, 28), (2, 11, 28), (0, 20, 31), (1, 17, 31), (2,
+    12, 31), (2, 13, 31), (0, 21, 34), (2, 14, 34), (1, 18, 34), (2, 15, 34), (0, 22, 37), (1, 19, 37), (2,
+    16, 37), (2, 17, 39), (0, 23, 40), (1, 20, 40), (2, 18, 40), (1, 21, 42), (2, 19, 44), (1, 22, 45), (2,
+    20, 46), (1, 23, 47), (2, 21, 47), (2, 22, 52), (2, 23, 55)
+)
+OUTER = (
+    (1, 0, 10), (1, 1, 12), (1, 2, 14), (1, 3, 14), (1, 4, 14), (1, 5, 14), (1, 6, 17), (1, 7, 19), (1, 8,
+    21), (2, 0, 21), (2, 1, 21), (1, 9, 23), (2, 2, 23), (2, 3, 23), (2, 4, 24), (1, 10, 24), (2, 5, 24), (2,
+    6, 24), (1, 11, 24), (2, 7, 24), (2, 8, 24), (1, 12, 24), (2, 9, 24), (2, 10, 24), (1, 13, 24), (2, 11,
+    24), (1, 14, 24), (2, 12, 24), (1, 15, 25), (2, 13, 27), (1, 16, 29), (2, 14, 31), (1, 17, 33), (2, 15,
+    35), (1, 18, 37), (2, 16, 39), (1, 19, 40), (2, 17, 40), (1, 20, 42), (2, 18, 44), (1, 21, 45), (2, 19,
+    46), (1, 22, 47), (2, 20, 48), (1, 23, 50), (2, 21, 52), (2, 22, 54), (2, 23, 59)
+)
 
 
 def exchange(
-    pieces, panel, front_cols, ids_hbm, arc_hbm, counts, inverse_hbm, front,
+    panel, front_cols, ids_hbm, arc_hbm, counts, inverse_hbm, front,
     cols, high, low, held, factor_part,
     blk, tile, inv_diag, inv_off, ids, arc_weight, inverse_rows,
     panels, scaled, weights, outgoing, from_outer, from_inner, own,
@@ -107,12 +124,13 @@
     def _():
         pl.semaphore_signal(barrier, inc=1, device_id={"obs": other}, device_id_type=MESH)
 
+    count, side_pieces = blk.shape[0], tile.shape[0]
+    wide = blk.shape[2]
+
     def load_front(c):
-        start, wide = pieces[c]
-        at = (slice(None), pl.ds(start, wide))
+        at = (slice(None), pl.ds(c * wide, wide))
         return pltpu.make_async_copy(front_cols.at[at], scaled.at[at], front_sem.at[c])
 
-    count = len(pieces)
     load_inverse = pltpu.make_async_copy(inverse_hbm, inverse_rows, local_sem.at[0])
     load_ids = pltpu.make_async_copy(ids_hbm, ids, local_sem.at[1])
     load_arcs = pltpu.make_async_copy(arc_hbm, arc_weight, local_sem.at[2])
@@ -123,9 +141,7 @@
     load_arcs.start()
     load_front(0).start()
     load_panel.start()
-    for c in range(count // 2, count):
-        load_front(c).start()
-    for c in range(1, count // 2):
+    for r, c in UNITS[1:count]:
         load_front(c).start()
     load_held.start()
 
@@ -160,17 +176,16 @@
     def await_on(ref, sem):
         pltpu.make_async_copy(ref, ref, sem).wait()
 
+    first = jnp.where(team == 0, beside_x, beside_y)
+    second = jnp.where(team == 0, beside_y, beside_x)
+    top, bottom = pl.ds(0, rows // 2), pl.ds(rows // 2, rows // 2)
     panel_copies = [
-        remote(panel, panels.at[1], panel_send.at[0], panel_recv.at[0], {"grid": beside_x}),
-        remote(panel, panels.at[2], panel_send.at[1], panel_recv.at[1], {"grid": beside_y}),
+        remote(panel, panels.at[1], panel_send.at[0], panel_recv.at[0], {"grid": first}),
+        remote(panel, panels.at[2], panel_send.at[1], panel_recv.at[1], {"grid": second}),
+        remote(panels.at[1, top], panels.at[3, top], panel_send.at[2], panel_recv.at[2], {"grid": second}),
+        remote(panels.at[2, bottom], panels.at[3, bottom], panel_send.at[3], panel_recv.at[3], {"grid": first}),
     ]
-    for copy in panel_copies:
-        copy.start()
-    top, bottom = pl.ds(0, rows // 2), pl.ds(rows // 2, rows // 2)
-    panel_copies += [
-        remote(panels.at[1, top], panels.at[3, top], panel_send.at[2], panel_recv.at[2], {"grid": beside_y}),
-        remote(panels.at[2, bottom], panels.at[3, bottom], panel_send.at[3], panel_recv.at[3], {"grid": beside_x}),
-    ]
+    panel_copies[0].start()
 
     inv_parts = (
         (0, team == 0, lambda *at: inv_diag.at[(0,) + at]),
@@ -255,44 +270,52 @@
         weights[i * arcs:(i + 1) * arcs, :] = upright(jnp.where(slot < live, looked, 0.0))
 
     def scale(c):
-        start, wide = pieces[c]
+        at_cols = slice(c * wide, (c + 1) * wide)
         load_front(c).wait()
 
         @pl.loop(0, rows // step)
         def _(i):
             at = pl.ds(pl.multiple_of(i * step, step), step)
-            part = scaled[at, start:start + wide].astype(jnp.float32)
-            scaled[at, start:start + wide] = (part * weights[at, :]).astype(jnp.bfloat16)
-
-    units = [(0, 0), (0, count // 2)]
-    units += [(r, 0) for r in (1, 2, 3)] + [(r, count // 2) for r in (1, 2, 3)]
-    units += [(r, c) for k in range(1, count // 2) for c in (k, k + count // 2) for r in (0, 1, 2, 3)]
-    source = (grid, beside_x, beside_y, across)
-
-    def piece_at(c):
-        return pl.ds(pieces[c][0], pieces[c][1])
+            part = scaled[at, at_cols].astype(jnp.float32)
+            scaled[at, at_cols] = (part * weights[at, :]).astype(jnp.bfloat16)
+
+    def source(t, r):
+        if r == 0:
+            return grid
+        if r == 3:
+            return across
+        return jnp.where(t == r - 1, beside_x, beside_y)
+
+    def tile_source(t, r):
+        root = root_y * 2 + root_x
+        flip_x = root_y * 2 + (1 - root_x)
+        flip_y = (1 - root_y) * 2 + root_x
+        both = (1 - root_y) * 2 + (1 - root_x)
+        return (root, (flip_x, flip_y)[t], (flip_y, flip_x)[t], both)[r]
 
     def staged(r, c):
-        return pl.ds(r * width, width), piece_at(c)
+        return c, pl.ds(r * width, width)
 
     def block_rows(t, g):
         return pl.ds(pl.multiple_of((t * 4 + g) * width, width), width)
 
     def place(t, r, c):
-        return block_rows(t, source[r]), piece_at(c)
-
-    def tile_place(t, g, c):
-        return block_rows(t, g), pl.ds(pieces[c % (count // 2)][0], pieces[c][1])
+        return c, block_rows(t, source(t, r))
+
+    def tile_place(t, r, c):
+        return c % side_pieces, block_rows(t, tile_source(t, r))
 
     def slot_of(r, c):
-        return r * (count // 2) + c % (count // 2)
+        return r * side_pieces + c % side_pieces
+
+    def in_half(c):
+        return half == c // side_pieces
 
     def compute(u):
-        r, c = units[u]
+        r, c = UNITS[u]
         if r == 0:
             scale(c)
-        start, wide = pieces[c]
-        total = contract_rows(panels[r], scaled[:, start:start + wide])
+        total = contract_rows(panels[r], scaled[:, c * wide:(c + 1) * wide])
         at = staged(r, c)
 
         @pl.when(is_inner)
@@ -305,22 +328,21 @@
             remote(outgoing.at[at], from_outer.at[at], outer_send.at[u], outer_recv.at[u], {"obs": mate}).start()
 
     def middle(u):
-        at = staged(*units[u])
+        at = staged(*UNITS[u])
         await_on(from_outer.at[at], outer_recv.at[u])
         total = own[at] + from_outer[at].astype(jnp.float32)
         own[at] = total
         outgoing[at] = total.astype(jnp.bfloat16)
         remote(outgoing.at[at], from_inner.at[at], inner_send.at[u], inner_recv.at[u], {"obs": other}).start()
 
-    def spread(u):
-        r, c = units[u]
+    def spread_tile(u):
+        r, c = UNITS[u]
         ref = blk.at[place(team, r, c)]
-        remote(ref, ref, team_send.at[u], team_recv.at[u], {"team": partner}).start()
-
-        @pl.when(sends_tile & (half == c // (count // 2)))
+
+        @pl.when(sends_tile & in_half(c))
         def _():
             k = slot_of(r, c)
-            to = tile.at[tile_place(team, source[r], c)]
+            to = tile.at[c % side_pieces, block_rows(team, source(team, r))]
             remote(ref, to, tile_send.at[0, k], tile_recv.at[team, k], {"team": owner, "grid": beside_x}).start()
             remote(ref, to, tile_send.at[1, k], tile_recv.at[team, k], {"team": owner, "grid": beside_y}).start()
 
@@ -332,8 +354,14 @@
             def _():
                 remote(ref, to, tile_send.at[2, k], tile_recv.at[team, k], {"team": partner}).start()
 
+    def spread(u):
+        ref = blk.at[place(team, *UNITS[u])]
+        if u >= count:
+            spread_tile(u)
+        remote(ref, ref, team_send.at[u], team_recv.at[u], {"team": partner}).start()
+
     def finished_inner(u):
-        r, c = units[u]
+        r, c = UNITS[u]
         at = staged(r, c)
         await_on(from_inner.at[at], inner_recv.at[u])
         total = own[at] + from_inner[at].astype(jnp.float32)
@@ -341,166 +369,149 @@
         blk[spot] = total.astype(jnp.bfloat16)
         ref = blk.at[spot]
         remote(ref, ref, total_send.at[u], total_recv.at[u], {"obs": mate}).start()
+        spread(u)
 
     def finished_outer(u):
-        r, c = units[u]
-        await_on(blk.at[place(team, r, c)], total_recv.at[u])
-
-    def tile_source(r):
-        root = root_y * 2 + root_x
-        flip_x = root_y * 2 + (1 - root_x)
-        flip_y = (1 - root_y) * 2 + root_x
-        both = (1 - root_y) * 2 + (1 - root_x)
-        return (root, flip_x, flip_y, both)[r]
+        await_on(blk.at[place(team, *UNITS[u])], total_recv.at[u])
+        spread(u)
 
     def relay(u):
-        r, c = units[u]
+        r, c = UNITS[u]
         k = slot_of(r, c)
-        even = (r + c) % 2 == 0
-
-        @pl.when((at_x if even else at_y) & (half == c // (count // 2)))
+
+        @pl.when(at_x & in_half(c))
         def _():
             for t in (0, 1):
-                ref = tile.at[tile_place(t, tile_source(r), c)]
+                ref = tile.at[tile_place(t, r, c)]
                 await_on(ref, tile_recv.at[t, k])
-                remote(ref, ref, relay_send.at[t, k], tile_recv.at[t, k],
-                       {"grid": beside_y if even else beside_x}).start()
-
-    whole, columns = blk.shape
+                remote(ref, ref, relay_send.at[t, k], tile_recv.at[t, k], {"grid": beside_y}).start()
+
     slab = inverse_rows.shape[0]
     size = 2 * slab
-    blocks = whole // size
+    blocks = blk.shape[1] // size
     pair = team * lines + z
 
-    def factor_of(ref, at, r):
+    def factor_of(ref, c, r):
         t, inner = r * size // side, r * size % side
-        first, near = inner // slab, slice(r * size, (r + 1) * size)
-        ahead = inv_diag[t, first:first + 2].reshape((size, inv_diag.shape[4]))
-        total = ahead[:, side:side + 1].astype(jnp.float32) * ref[near, at].astype(jnp.float32)
+        begin, near = inner // slab, slice(r * size, (r + 1) * size)
+        ahead = inv_diag[t, begin:begin + 2].reshape((size, inv_diag.shape[4]))
+        total = ahead[:, side:side + 1].astype(jnp.float32) * ref[c, near].astype(jnp.float32)
         total += jnp.dot(
-            ahead[:, :inner + size], ref[t * side:t * side + inner + size, at],
+            ahead[:, :inner + size], ref[c, t * side:t * side + inner + size],
             preferred_element_type=jnp.float32,
         )
         if t:
-            behind = inv_off[first:first + 2].reshape((size, side))
-            total += jnp.dot(behind, ref[:side, at], preferred_element_type=jnp.float32)
+            behind = inv_off[begin:begin + 2].reshape((size, side))
+            total += jnp.dot(behind, ref[c, :side], preferred_element_type=jnp.float32)
         return total
 
-    def await_columns(c):
-        for u in range(last):
-            if units[u][1] == c:
-                await_on(blk.at[place(partner, *units[u])], team_recv.at[u])
-
     def factor_columns(c, r):
-        at = slice(pieces[c][0], pieces[c][0] + pieces[c][1])
-        value = factor_of(blk, at, r)
-        cols[r * size:(r + 1) * size, at] = value.astype(jnp.bfloat16)
+        if r == 0:
+            for u in range(len(UNITS)):
+                if UNITS[u][1] == c:
+                    await_on(blk.at[place(partner, *UNITS[u])], team_recv.at[u])
+        value = factor_of(blk, c, r)
+        cols[c, r * size:(r + 1) * size] = value.astype(jnp.bfloat16)
         for part in range(size // slab):
             @pl.when(pair == r * (size // slab) + part)
             def _():
-                factor_part[:, at] = value[part * slab:(part + 1) * slab]
-
-    def await_tile(c):
-        for u in range(last):
-            r, d = units[u]
-            if d % (count // 2) == c:
-                k = slot_of(r, d)
-                even = (r + d) % 2 == 0
-
-                @pl.when((half == d // (count // 2)) & jnp.logical_not(at_x if even else at_y))
-                def _():
-                    for t in (0, 1):
-                        await_on(tile.at[tile_place(t, tile_source(r), d)], tile_recv.at[t, k])
-
-    def factor_tile(c, r):
-        at = slice(pieces[c][0], pieces[c][0] + pieces[c][1])
-        value = factor_of(tile, at, r)
+                factor_part[:, c * wide:(c + 1) * wide] = value[part * slab:(part + 1) * slab]
+
+    def factor_tile(j, r):
+        if r == 0:
+            for d, c in UNITS:
+                if c % side_pieces == j:
+                    @pl.when(in_half(c) & jnp.logical_not(at_x))
+                    def _():
+                        for t in (0, 1):
+                            await_on(tile.at[tile_place(t, d, c)], tile_recv.at[t, slot_of(d, c)])
+        value = factor_of(tile, j, r)
         upper = value.astype(jnp.bfloat16)
-        high[r * size:(r + 1) * size, at] = upper
-        low[r * size:(r + 1) * size, at] = (value - upper.astype(jnp.float32)).astype(jnp.bfloat16)
-
-    def update(c, part):
-        at = slice(pieces[c][0], pieces[c][0] + pieces[c][1])
-        near = slice(part * size, (part + 1) * size)
-        change = contract_rows(high[:, near], cols[:, at]) + contract_rows(low[:, near], cols[:, at])
+        high[j, r * size:(r + 1) * size] = upper
+        low[j, r * size:(r + 1) * size] = (value - upper.astype(jnp.float32)).astype(jnp.bfloat16)
+
+    def update(c, j):
+        near, at = slice(j * wide, (j + 1) * wide), slice(c * wide, (c + 1) * wide)
+        change = contract_rows(high[j], cols[c]) + contract_rows(low[j], cols[c])
         held[near, at] = held[near, at] - change
 
-    last = len(units)
-    far = count // 2
-    tasks = {
-        10: [lambda: inv_team("wait"), lambda: await_columns(0)] + [lambda r=r: factor_columns(0, r) for r in range(blocks - 1)],
-        11: [lambda: factor_columns(0, blocks - 1)],
-        13: [lambda: await_columns(far)] + [lambda r=r: factor_columns(far, r) for r in range(blocks - 1)],
-        14: [lambda: factor_columns(far, blocks - 1)],
-        17: [lambda: await_columns(1)] + [lambda r=r: factor_columns(1, r) for r in range(blocks)],
-        18: [lambda: await_tile(0)] + [lambda r=r: factor_tile(0, r) for r in range(blocks - 1)],
-        19: [lambda: factor_tile(0, blocks - 1), load_held.wait],
-        20: [lambda: update(0, 0)],
-        21: [lambda: update(0, 1)],
-        22: [lambda: update(far, 0)],
-        23: [lambda: update(far, 1), lambda: update(1, 0), lambda: update(1, 1)],
-        24: [lambda: await_columns(far + 1)] + [lambda r=r: factor_columns(far + 1, r) for r in range(blocks)],
-        25: [lambda: await_tile(1)] + [lambda r=r: factor_tile(1, r) for r in range(blocks)],
-    }
-    for i in range(last + 10):
+    last = len(UNITS)
+    work = [(compute, (u,)) for u in range(last)]
+
+    def columns_work(c):
+        return [(factor_columns, (c, r)) for r in range(blocks)]
+
+    def tile_work(j):
+        return [(factor_tile, (j, r)) for r in range(blocks)]
+
+    def update_work(cs, js):
+        return [(update, (c, j)) for j in js for c in cs]
+
+    work += columns_work(0) + columns_work(3) + columns_work(1) + columns_work(4)
+    work += tile_work(0) + update_work((0, 3, 1, 4), (0,))
+    work += tile_work(1) + update_work((0, 3), (1,)) + columns_work(2) + update_work((1, 4), (1,))
+    work += update_work((2,), (0, 1)) + columns_work(5) + tile_work(2)
+    starts = [min(u for u in range(last) if UNITS[u][0] == r) for r in range(4)]
+
+    def hooks(i):
         if i == 0:
             load_panel.wait()
-        if i == 1:
+        if i == 2:
             inv_line(0, "wait")
             inv_line(1, "start")
-        if i == 2:
+        if i == 4:
             inv_line(1, "wait")
             inv_line(2, "start")
-        if i == 3:
+        if i == 5:
+            panel_copies[0].wait_send()
+            panel_copies[1].start()
+        if i == starts[1]:
             inv_line(2, "wait")
+            panel_copies[0].wait_recv()
+            panel_copies[2].start()
+        if i == starts[2]:
+            panel_copies[1].wait_recv()
+            panel_copies[3].start()
             inv_grid(0, "start")
-        if i == 6:
+        if i == starts[3]:
+            panel_copies[2].wait_recv()
+            panel_copies[3].wait_recv()
+        if i == starts[3] + 1:
+            for u in range(count):
+                spread_tile(u)
+        if i == starts[3] + 5:
             inv_grid(0, "wait")
             inv_grid(1, "start")
-        if i == 8:
+        if i == starts[3] + 8:
             inv_grid(1, "wait")
             inv_team("start")
-
-        @pl.when(is_inner)
-        def _():
-            if 0 <= i - 1 < last:
-                middle(i - 1)
-            if 0 <= i - 3 < last:
-                finished_inner(i - 3)
-                spread(i - 3)
-
-        if i == 2:
-            panel_copies[0].wait_recv()
-            panel_copies[2].start()
-            panel_copies[1].wait_recv()
-            panel_copies[3].start()
-        if i == 4:
-            panel_copies[2].wait_recv()
-            panel_copies[3].wait_recv()
-
-        if i < last:
-            compute(i)
-
-        @pl.when(is_outer)
-        def _():
-            if 0 <= i - 5 < last:
-                finished_outer(i - 5)
-                spread(i - 5)
-
-        @pl.when(is_inner)
-        def _():
-            if 0 <= i - 5 < last:
-                relay(i - 5)
-
-        @pl.when(is_outer)
-        def _():
-            if 0 <= i - 7 < last:
-                relay(i - 7)
-
-        for task in tasks.get(i, ()):
-            task()
-
-    for copy in panel_copies:
+        if i == last:
+            inv_team("wait")
+        if i == last + 5 * blocks:
+            load_held.wait()
+
+    def role_work(steps, functions, i):
+        for kind, u, at in steps:
+            if at == i:
+                functions[kind](u)
+
+    for i in range(len(work) + 1):
+        if any(at == i for _, _, at in INNER):
+            @pl.when(is_inner)
+            def _():
+                role_work(INNER, (middle, finished_inner, relay), i)
+
+        if any(at == i for _, _, at in OUTER):
+            @pl.when(is_outer)
+            def _():
+                role_work(OUTER, (None, finished_outer, relay), i)
+
+        hooks(i)
+        if i < len(work):
+            function, at = work[i]
+            function(*at)
+
+    for copy in (panel_copies[1], panel_copies[2], panel_copies[3]):
         copy.wait_send()
     for s in range(lines - 1):
         inv_line(s, "drain")
@@ -508,11 +519,9 @@
     inv_grid(1, "drain")
     inv_team("drain")
     for u in range(last):
-        r, c = units[u]
+        r, c = UNITS[u]
         k = slot_of(r, c)
         at = staged(r, c)
-        in_half = half == c // (count // 2)
-        even = (r + c) % 2 == 0
         ref = blk.at[place(team, r, c)]
         await_on(ref, team_send.at[u])
 
@@ -525,7 +534,7 @@
             await_on(outgoing.at[at], inner_send.at[u])
             await_on(ref, total_send.at[u])
 
-        @pl.when(in_half & sends_tile)
+        @pl.when(in_half(c) & sends_tile)
         def _():
             await_on(ref, tile_send.at[0, k])
             await_on(ref, tile_send.at[1, k])
@@ -534,38 +543,34 @@
             def _():
                 await_on(ref, tile_send.at[2, k])
 
-        @pl.when(in_half & (at_x if even else at_y))
+        @pl.when(in_half(c) & at_x)
         def _():
             for t in (0, 1):
-                await_on(tile.at[tile_place(t, tile_source(r), c)], relay_send.at[t, k])
-
-
-def finish(pieces, cols, high, low, held, factor_part, factor_out, front_out, done, sems):
-    count = len(pieces)
-    tile_rows, columns = held.shape
-    wide = pieces[0][1]
-    ready = [0, count // 2, 1]
+                await_on(tile.at[tile_place(t, r, c)], relay_send.at[t, k])
+
+
+def finish(cols, high, low, held, factor_part, factor_out, front_out, done, sems):
+    count, side_pieces = cols.shape[0], high.shape[0]
+    wide = cols.shape[2]
+    near = (side_pieces - 1) * wide
     copies = [pltpu.make_async_copy(factor_part, factor_out, sems.at[0])]
-
-    def store(ref, near, start, width):
-        at = (pl.ds(near[0], near[1]), pl.ds(start, width))
-        copies.append(pltpu.make_async_copy(ref.at[at], front_out.at[at], sems.at[len(copies)]))
+    at = (pl.ds(0, near), pl.ds(0, (count - 1) * wide))
+    copies.append(pltpu.make_async_copy(held.at[at], front_out.at[at], sems.at[1]))
+    for copy in copies:
+        copy.start()
+
+    def update(j, c):
+        rows, columns = slice(j * wide, (j + 1) * wide), slice(c * wide, (c + 1) * wide)
+        change = contract_rows(high[j], cols[c]) + contract_rows(low[j], cols[c])
+        done[rows, columns] = held[rows, columns] - change
+        at = (pl.ds(j * wide, wide), pl.ds(c * wide, wide))
+        copies.append(pltpu.make_async_copy(done.at[at], front_out.at[at], sems.at[len(copies)]))
         copies[-1].start()
 
-    copies[0].start()
-    for c in ready:
-        store(held, (0, wide), *pieces[c])
-
-    def update(near, start, width):
-        rows, at = slice(near[0], near[0] + near[1]), slice(start, start + width)
-        change = contract_rows(high[:, rows], cols[:, at]) + contract_rows(low[:, rows], cols[:, at])
-        done[rows, at] = held[rows, at] - change
-        store(done, near, start, width)
-
-    final = pieces[count // 2 + 1]
-    update((0, wide), *final)
-    for start, width in pieces[0::2] + pieces[1::2]:
-        update((wide, tile_rows - wide), start, width)
+    for j in range(side_pieces - 1):
+        update(j, count - 1)
+    for c in range(count):
+        update(side_pieces - 1, c)
     for copy in copies:
         copy.wait()
 
@@ -578,7 +583,8 @@
     tile_rows = front.shape[0]
     side = whole // 2
     share = slab // grids
-    pieces = column_pieces(cols, tile_rows)
+    wide = tile_rows // 3
+    count = cols // wide
     vmem = pl.BlockSpec(memory_space=pltpu.VMEM)
     smem = pl.BlockSpec(memory_space=pltpu.SMEM)
     hbm = pl.BlockSpec(memory_space=pltpu.HBM)
@@ -589,23 +595,23 @@
     def stay(value):
         return pltpu.with_memory_space_constraint(value, pltpu.HBM)
 
-    units = grids * len(pieces)
+    units = grids * count
     slots = units // 2
     f32 = jnp.float32
     outs = pl.pallas_call(
-        functools.partial(exchange, pieces),
+        exchange,
         out_shape=(
-            jax.ShapeDtypeStruct((whole, cols), bf16),
-            jax.ShapeDtypeStruct((whole, tile_rows), bf16),
-            jax.ShapeDtypeStruct((whole, tile_rows), bf16),
+            jax.ShapeDtypeStruct((count, whole, wide), bf16),
+            jax.ShapeDtypeStruct((3, whole, wide), bf16),
+            jax.ShapeDtypeStruct((3, whole, wide), bf16),
             jax.ShapeDtypeStruct(front.shape, f32),
             jax.ShapeDtypeStruct((slab, cols), f32),
         ),
         in_specs=[hbm, hbm, hbm, hbm, smem, hbm, hbm],
         out_specs=(vmem,) * 5,
         scratch_shapes=[
-            pltpu.VMEM((whole, cols), bf16),
-            pltpu.VMEM((whole, tile_rows), bf16),
+            pltpu.VMEM((count, whole, wide), bf16),
+            pltpu.VMEM((3, whole, wide), bf16),
             pltpu.VMEM((2, lines, grids, share, side + 128), bf16),
             pltpu.VMEM((lines, grids, share, side), bf16),
             pltpu.VMEM((rows // arcs, arcs), jnp.int32),
@@ -614,11 +620,11 @@
             pltpu.VMEM((grids, rows, width), bf16),
             pltpu.VMEM((rows, cols), bf16),
             pltpu.VMEM((rows, 1), f32),
-            pltpu.VMEM((grids * width, cols), bf16),
-            pltpu.VMEM((grids * width, cols), bf16),
-            pltpu.VMEM((grids * width, cols), bf16),
-            pltpu.VMEM((grids * width, cols), f32),
-            dma((len(pieces),)), dma((5,)), dma((4,)), dma((4,)),
+            pltpu.VMEM((count, grids * width, wide), bf16),
+            pltpu.VMEM((count, grids * width, wide), bf16),
+            pltpu.VMEM((count, grids * width, wide), bf16),
+            pltpu.VMEM((count, grids * width, wide), f32),
+            dma((count,)), dma((5,)), dma((4,)), dma((4,)),
             dma((units,)), dma((units,)), dma((units,)), dma((units,)),
             dma((units,)), dma((units,)), dma((units,)), dma((units,)),
             dma((3, slots)), dma((2, slots)), dma((2, slots)),
@@ -631,7 +637,7 @@
     )(stay(design_panel), stay(design_front), stay(arc_ids.reshape((rows // arcs, arcs))),
       stay(arc_weight[None, :]), row_counts, stay(panel_inverse), stay(front))
     return pl.pallas_call(
-        functools.partial(finish, pieces),
+        finish,
         out_shape=(
             jax.ShapeDtypeStruct((slab, cols), f32),
             jax.ShapeDtypeStruct(front.shape, f32),
@@ -640,7 +646,7 @@
         out_specs=(hbm, hbm),
         scratch_shapes=[
             pltpu.VMEM(front.shape, f32),
-            dma((2 * len(pieces) + 1,)),
+            dma((count + 4,)),
         ],
         compiler_params=pltpu.CompilerParams(vmem_limit_bytes=12 * 2**20),
         name="finish",

time: 77.6 us -> 75.5 us (0.973)
  Pallas kernels: 76 us -> 73.8 us
    pallas_call x2, Pallas kernels: 76 us -> 73.8 us  [the longest x1 70.4 us: local_kernels(): pl.pallas_call(exchange, out_shape=(jax.ShapeDtypeStruct((count, whole, w...]
where the time goes in v3:
time: 75.5 us; the launch traced here: 75.3 us
  Pallas kernels  73.8 us (98%)
  between operations  1.47 us (2%)
    pallas_call x1, Pallas kernels, local_kernels(): pl.pallas_call(exchange, out_shape=(jax.ShapeDtypeStruct((count, whole, w...  70.4 us
    pallas_call x1, Pallas kernels, local_kernels(): pl.pallas_call(finish, out_shape=(jax.ShapeDtypeStruct((slab, cols), f32)...  3.4 us

profile of v3, /device:TPU:0, one launch (start us, length us, event | category | flops | bytes accessed | tf_op | source)
XLA Modules:
  0.0 75.3 jit_solution(493796505275996215)
XLA Ops:
  1.3 70.4 %exchange.1 = (bf16[6,1024,256]{2,1,0:T(8,128)(2,1)S(1)}, bf16[3,1024,256]{2,1,0:T(8,128)(2,1)S(1)}, bf16[3,1024,256]{2,1,0:T(8,128)(2,1)S(1)}, f32[768,1536]{1,0:T(8,128)S(1)}, f32[128,1536]{1,0:T(8,128)S(1)}) custom-call(bf16[2048,128]{1,0:T(8,128)(2,1)} %panel.1, bf16[2048,1536]{1,0:T(8,128)(2,1)} %front_cols.1, s32[16,128]{1,0:T(8,128)} %bitcast.2, ...), custom_call_target="tpu_custom_call" | custom-call | tf_op jit(solution)/shard_map/exchange/pallas_call | solution.py:601
  71.7 3.4 %finish.1 = (f32[128,1536]{1,0:T(8,128)}, f32[768,1536]{1,0:T(8,128)}) custom-call(bf16[6,1024,256]{2,1,0:T(8,128)(2,1)S(1)} %get-tuple-element.7.cols, bf16[3,1024,256]{2,1,0:T(8,128)(2,1)S(1)} %get-tuple-element.8.high, bf16[3,1024,256]{2,1,0:T(8,128)(2,1)S(1)} %get-tuple-element.9.low, f32[768,1536]{1,0:T(8,128)S(1)} %get-tuple-element.10.held, ...), custom_call_target="tpu_custom_call" | custom-call | tf_op jit(solution)/shard_map/finish/pallas_call | solution.py:639

commit v4 on v3

--- a/solution.py
+++ b/solution.py
@@ -55,28 +55,28 @@
 MESH = pl.DeviceIdType.MESH
 
 
+DIRECT = 18
 UNITS = (
     (0, 0), (0, 3), (0, 1), (0, 4), (0, 2), (0, 5), (1, 0), (1, 3), (1, 1), (1, 4), (2, 0), (2, 3), (2, 1),
     (2, 4), (3, 0), (3, 3), (3, 1), (3, 4), (1, 2), (2, 2), (3, 2), (1, 5), (2, 5), (3, 5)
 )
 INNER = (
-    (0, 0, 4), (0, 1, 6), (0, 2, 7), (1, 0, 8), (0, 3, 8), (0, 4, 10), (1, 1, 10), (0, 5, 10), (1, 2, 10), (0,
+    (0, 0, 4), (0, 1, 5), (0, 2, 6), (0, 3, 8), (1, 0, 8), (0, 4, 9), (1, 1, 9), (0, 5, 10), (1, 2, 10), (0,
     6, 10), (1, 3, 11), (0, 7, 12), (1, 4, 12), (0, 8, 14), (1, 5, 14), (0, 9, 14), (1, 6, 14), (0, 10, 14),
-    (1, 7, 14), (0, 11, 14), (1, 8, 15), (0, 12, 16), (1, 9, 16), (0, 13, 18), (1, 10, 18), (0, 14, 19), (2,
-    0, 19), (1, 11, 19), (2, 1, 19), (0, 15, 21), (1, 12, 21), (2, 2, 21), (2, 3, 21), (0, 16, 22), (1, 13,
-    22), (2, 4, 22), (2, 5, 22), (0, 17, 23), (2, 6, 23), (1, 14, 23), (2, 7, 23), (2, 8, 24), (0, 18, 24),
-    (1, 15, 24), (2, 9, 24), (0, 19, 28), (1, 16, 28), (2, 10, 28), (2, 11, 28), (0, 20, 31), (1, 17, 31), (2,
-    12, 31), (2, 13, 31), (0, 21, 34), (2, 14, 34), (1, 18, 34), (2, 15, 34), (0, 22, 37), (1, 19, 37), (2,
-    16, 37), (2, 17, 39), (0, 23, 40), (1, 20, 40), (2, 18, 40), (1, 21, 42), (2, 19, 44), (1, 22, 45), (2,
-    20, 46), (1, 23, 47), (2, 21, 47), (2, 22, 52), (2, 23, 55)
+    (1, 7, 14), (0, 11, 15), (1, 8, 15), (0, 12, 16), (1, 9, 17), (0, 13, 18), (1, 10, 18), (0, 14, 19), (1,
+    11, 20), (2, 0, 20), (2, 1, 20), (0, 15, 21), (1, 12, 21), (2, 2, 21), (2, 3, 21), (0, 16, 22), (1, 13,
+    22), (2, 4, 22), (2, 5, 22), (0, 17, 23), (1, 14, 23), (2, 6, 24), (0, 18, 24), (2, 7, 24), (1, 15, 24),
+    (2, 8, 25), (2, 9, 25), (0, 19, 27), (1, 16, 28), (2, 10, 28), (2, 11, 28), (0, 20, 30), (1, 17, 31), (2,
+    12, 31), (2, 13, 31), (0, 21, 32), (1, 18, 34), (2, 14, 35), (2, 15, 35), (0, 22, 36), (1, 19, 37), (2,
+    16, 39), (0, 23, 40), (1, 20, 40), (2, 17, 40), (1, 21, 40), (1, 22, 40), (1, 23, 45)
 )
 OUTER = (
-    (1, 0, 10), (1, 1, 12), (1, 2, 14), (1, 3, 14), (1, 4, 14), (1, 5, 14), (1, 6, 17), (1, 7, 19), (1, 8,
-    21), (2, 0, 21), (2, 1, 21), (1, 9, 23), (2, 2, 23), (2, 3, 23), (2, 4, 24), (1, 10, 24), (2, 5, 24), (2,
-    6, 24), (1, 11, 24), (2, 7, 24), (2, 8, 24), (1, 12, 24), (2, 9, 24), (2, 10, 24), (1, 13, 24), (2, 11,
-    24), (1, 14, 24), (2, 12, 24), (1, 15, 25), (2, 13, 27), (1, 16, 29), (2, 14, 31), (1, 17, 33), (2, 15,
-    35), (1, 18, 37), (2, 16, 39), (1, 19, 40), (2, 17, 40), (1, 20, 42), (2, 18, 44), (1, 21, 45), (2, 19,
-    46), (1, 22, 47), (2, 20, 48), (1, 23, 50), (2, 21, 52), (2, 22, 54), (2, 23, 59)
+    (1, 0, 12), (1, 1, 14), (1, 2, 14), (1, 3, 14), (1, 4, 14), (1, 5, 17), (1, 6, 19), (1, 7, 21), (2, 0,
+    22), (2, 1, 22), (1, 8, 22), (2, 2, 24), (2, 3, 24), (1, 9, 24), (2, 4, 24), (2, 5, 24), (1, 10, 24), (2,
+    6, 24), (2, 7, 24), (1, 11, 24), (2, 8, 24), (1, 12, 24), (2, 9, 24), (1, 13, 24), (2, 10, 24), (1, 14,
+    24), (2, 11, 24), (1, 15, 24), (2, 12, 26), (1, 16, 29), (2, 13, 30), (1, 17, 32), (2, 14, 34), (1, 18,
+    37), (2, 15, 38), (1, 19, 40), (2, 16, 40), (1, 20, 40), (2, 17, 40), (1, 21, 40), (1, 22, 44), (1, 23,
+    46)
 )
 
 
@@ -108,15 +108,13 @@
     owner = y
     sends_tile = x == root_x
     root_y = team
-    is_root = (x == root_x) & (y == root_y)
     at_x = (x != root_x) & (y == root_y)
-    at_y = (x == root_x) & (y != root_y)
-    at_across = (x != root_x) & (y != root_y)
 
     barrier = pltpu.get_barrier_semaphore()
     for where in (
         {"grid": beside_x}, {"grid": beside_y}, {"team": partner}, {"obs": mate},
         {"team": partner, "grid": beside_x}, {"team": partner, "grid": beside_y},
+        {"grid": across}, {"team": partner, "grid": across},
     ):
         pl.semaphore_signal(barrier, inc=1, device_id=where, device_id_type=MESH)
 
@@ -165,7 +163,7 @@
 
     inv_diag[team, z, grid, :, side:] = rest
 
-    pl.semaphore_wait(barrier, jnp.where(is_inner, 7, 6))
+    pl.semaphore_wait(barrier, jnp.where(is_inner, 9, 8))
 
     def remote(src, dst, send, recv, where):
         return pltpu.make_async_remote_copy(
@@ -267,7 +265,7 @@
         hit = ids[i:i + 1, :] == place_of
         looked = jnp.sum(jnp.where(hit, arc_column, 0.0), axis=0, keepdims=True)
         slot = lax.broadcasted_iota(jnp.int32, (1, arcs), 1) + i * arcs
-        weights[i * arcs:(i + 1) * arcs, :] = upright(jnp.where(slot < live, looked, 0.0))
+        weights[i * arcs:(i + 1) * arcs, :] = jnp.broadcast_to(upright(jnp.where(slot < live, looked, 0.0)), (arcs, arcs))
 
     def scale(c):
         at_cols = slice(c * wide, (c + 1) * wide)
@@ -276,8 +274,9 @@
         @pl.loop(0, rows // step)
         def _(i):
             at = pl.ds(pl.multiple_of(i * step, step), step)
+            factor = jnp.concatenate([weights[at, :]] * (wide // weights.shape[1]), axis=1)
             part = scaled[at, at_cols].astype(jnp.float32)
-            scaled[at, at_cols] = (part * weights[at, :]).astype(jnp.bfloat16)
+            scaled[at, at_cols] = (part * factor).astype(jnp.bfloat16)
 
     def source(t, r):
         if r == 0:
@@ -345,6 +344,8 @@
             to = tile.at[c % side_pieces, block_rows(team, source(team, r))]
             remote(ref, to, tile_send.at[0, k], tile_recv.at[team, k], {"team": owner, "grid": beside_x}).start()
             remote(ref, to, tile_send.at[1, k], tile_recv.at[team, k], {"team": owner, "grid": beside_y}).start()
+            if u >= DIRECT:
+                remote(ref, to, tile_send.at[3, k], tile_recv.at[team, k], {"team": owner, "grid": across}).start()
 
             @pl.when(team == owner)
             def _():
@@ -419,9 +420,9 @@
 
     def factor_tile(j, r):
         if r == 0:
-            for d, c in UNITS:
+            for u, (d, c) in enumerate(UNITS):
                 if c % side_pieces == j:
-                    @pl.when(in_half(c) & jnp.logical_not(at_x))
+                    @pl.when(in_half(c) & (jnp.logical_not(at_x) | (u >= DIRECT)))
                     def _():
                         for t in (0, 1):
                             await_on(tile.at[tile_place(t, d, c)], tile_recv.at[t, slot_of(d, c)])
@@ -451,6 +452,7 @@
     work += tile_work(0) + update_work((0, 3, 1, 4), (0,))
     work += tile_work(1) + update_work((0, 3), (1,)) + columns_work(2) + update_work((1, 4), (1,))
     work += update_work((2,), (0, 1)) + columns_work(5) + tile_work(2)
+    early = max(at for kind, u, at in INNER + OUTER if kind == 1 and u < count)
     starts = [min(u for u in range(last) if UNITS[u][0] == r) for r in range(4)]
 
     def hooks(i):
@@ -462,8 +464,7 @@
         if i == 4:
             inv_line(1, "wait")
             inv_line(2, "start")
-        if i == 5:
-            panel_copies[0].wait_send()
+        if i == 3:
             panel_copies[1].start()
         if i == starts[1]:
             inv_line(2, "wait")
@@ -476,7 +477,7 @@
         if i == starts[3]:
             panel_copies[2].wait_recv()
             panel_copies[3].wait_recv()
-        if i == starts[3] + 1:
+        if i == early:
             for u in range(count):
                 spread_tile(u)
         if i == starts[3] + 5:
@@ -511,7 +512,7 @@
             function, at = work[i]
             function(*at)
 
-    for copy in (panel_copies[1], panel_copies[2], panel_copies[3]):
+    for copy in panel_copies:
         copy.wait_send()
     for s in range(lines - 1):
         inv_line(s, "drain")
@@ -538,15 +539,18 @@
         def _():
             await_on(ref, tile_send.at[0, k])
             await_on(ref, tile_send.at[1, k])
+            if u >= DIRECT:
+                await_on(ref, tile_send.at[3, k])
 
             @pl.when(team != owner)
             def _():
                 await_on(ref, tile_send.at[2, k])
 
-        @pl.when(in_half(c) & at_x)
-        def _():
-            for t in (0, 1):
-                await_on(tile.at[tile_place(t, r, c)], relay_send.at[t, k])
+        if u < DIRECT:
+            @pl.when(in_half(c) & at_x)
+            def _():
+                for t in (0, 1):
+                    await_on(tile.at[tile_place(t, r, c)], relay_send.at[t, k])
 
 
 def finish(cols, high, low, held, factor_part, factor_out, front_out, done, sems):
@@ -619,7 +623,7 @@
             pltpu.VMEM((slab, whole), f32),
             pltpu.VMEM((grids, rows, width), bf16),
             pltpu.VMEM((rows, cols), bf16),
-            pltpu.VMEM((rows, 1), f32),
+            pltpu.VMEM((rows, arcs), f32),
             pltpu.VMEM((count, grids * width, wide), bf16),
             pltpu.VMEM((count, grids * width, wide), bf16),
             pltpu.VMEM((count, grids * width, wide), bf16),
@@ -627,7 +631,7 @@
             dma((count,)), dma((5,)), dma((4,)), dma((4,)),
             dma((units,)), dma((units,)), dma((units,)), dma((units,)),
             dma((units,)), dma((units,)), dma((units,)), dma((units,)),
-            dma((3, slots)), dma((2, slots)), dma((2, slots)),
+            dma((4, slots)), dma((2, slots)), dma((2, slots)),
             dma((3, 2, hops)), dma((3, 2, hops)), dma((3, 4)), dma((3, 4)), dma((3,)), dma((3,)),
         ],
         compiler_params=pltpu.CompilerParams(

time: 75.5 us -> 71.4 us (0.946)
  Pallas kernels: 73.8 us -> 69.8 us
    pallas_call x1, Pallas kernels: 70.4 us -> 66.4 us  [local_kernels(): pl.pallas_call(exchange, out_shape=(jax.ShapeDtypeStruct((count, whole, w...]
where the time goes in v4:
time: 71.4 us; the launch traced here: 71.3 us
  Pallas kernels  69.8 us (98%)
  between operations  1.45 us (2%)
    pallas_call x1, Pallas kernels, local_kernels(): pl.pallas_call(exchange, out_shape=(jax.ShapeDtypeStruct((count, whole, w...  66.4 us
    pallas_call x1, Pallas kernels, local_kernels(): pl.pallas_call(finish, out_shape=(jax.ShapeDtypeStruct((slab, cols), f32)...  3.39 us

profile of v4, /device:TPU:0, one launch (start us, length us, event | category | flops | bytes accessed | tf_op | source)
XLA Modules:
  0.0 71.3 jit_solution(10625248239239930697)
XLA Ops:
  1.3 66.4 %exchange.1 = (bf16[6,1024,256]{2,1,0:T(8,128)(2,1)S(1)}, bf16[3,1024,256]{2,1,0:T(8,128)(2,1)S(1)}, bf16[3,1024,256]{2,1,0:T(8,128)(2,1)S(1)}, f32[768,1536]{1,0:T(8,128)S(1)}, f32[128,1536]{1,0:T(8,128)S(1)}) custom-call(bf16[2048,128]{1,0:T(8,128)(2,1)} %panel.1, bf16[2048,1536]{1,0:T(8,128)(2,1)} %front_cols.1, s32[16,128]{1,0:T(8,128)} %bitcast.2, ...), custom_call_target="tpu_custom_call" | custom-call | tf_op jit(solution)/shard_map/exchange/pallas_call | solution.py:605
  67.7 3.4 %finish.1 = (f32[128,1536]{1,0:T(8,128)}, f32[768,1536]{1,0:T(8,128)}) custom-call(bf16[6,1024,256]{2,1,0:T(8,128)(2,1)S(1)} %get-tuple-element.7.cols, bf16[3,1024,256]{2,1,0:T(8,128)(2,1)S(1)} %get-tuple-element.8.high, bf16[3,1024,256]{2,1,0:T(8,128)(2,1)S(1)} %get-tuple-element.9.low, f32[768,1536]{1,0:T(8,128)S(1)} %get-tuple-element.10.held, ...), custom_call_target="tpu_custom_call" | custom-call | tf_op jit(solution)/shard_map/finish/pallas_call | solution.py:643

commit v5 on v4

--- a/solution.py
+++ b/solution.py
@@ -68,21 +68,22 @@
     22), (2, 4, 22), (2, 5, 22), (0, 17, 23), (1, 14, 23), (2, 6, 24), (0, 18, 24), (2, 7, 24), (1, 15, 24),
     (2, 8, 25), (2, 9, 25), (0, 19, 27), (1, 16, 28), (2, 10, 28), (2, 11, 28), (0, 20, 30), (1, 17, 31), (2,
     12, 31), (2, 13, 31), (0, 21, 32), (1, 18, 34), (2, 14, 35), (2, 15, 35), (0, 22, 36), (1, 19, 37), (2,
-    16, 39), (0, 23, 40), (1, 20, 40), (2, 17, 40), (1, 21, 40), (1, 22, 40), (1, 23, 45)
+    16, 39), (2, 18, 39), (0, 23, 40), (1, 20, 40), (2, 17, 40), (1, 21, 40), (1, 22, 40), (2, 19, 42), (1,
+    23, 45), (2, 20, 45), (2, 21, 45), (2, 22, 45), (2, 23, 50)
 )
 OUTER = (
     (1, 0, 12), (1, 1, 14), (1, 2, 14), (1, 3, 14), (1, 4, 14), (1, 5, 17), (1, 6, 19), (1, 7, 21), (2, 0,
     22), (2, 1, 22), (1, 8, 22), (2, 2, 24), (2, 3, 24), (1, 9, 24), (2, 4, 24), (2, 5, 24), (1, 10, 24), (2,
     6, 24), (2, 7, 24), (1, 11, 24), (2, 8, 24), (1, 12, 24), (2, 9, 24), (1, 13, 24), (2, 10, 24), (1, 14,
     24), (2, 11, 24), (1, 15, 24), (2, 12, 26), (1, 16, 29), (2, 13, 30), (1, 17, 32), (2, 14, 34), (1, 18,
-    37), (2, 15, 38), (1, 19, 40), (2, 16, 40), (1, 20, 40), (2, 17, 40), (1, 21, 40), (1, 22, 44), (1, 23,
-    46)
+    37), (2, 15, 38), (1, 19, 40), (2, 16, 40), (1, 20, 40), (2, 17, 40), (1, 21, 40), (2, 18, 42), (1, 22,
+    44), (2, 19, 45), (2, 20, 45), (2, 21, 45), (1, 23, 46), (2, 22, 49), (2, 23, 51)
 )
 
 
 def exchange(
     panel, front_cols, ids_hbm, arc_hbm, counts, inverse_hbm, front,
-    cols, high, low, held, factor_part,
+    cols, both, held, factor_part,
     blk, tile, inv_diag, inv_off, ids, arc_weight, inverse_rows,
     panels, scaled, weights, outgoing, from_outer, from_inner, own,
     front_sem, local_sem, panel_send, panel_recv, outer_send, outer_recv, inner_send, inner_recv,
@@ -109,6 +110,7 @@
     sends_tile = x == root_x
     root_y = team
     at_x = (x != root_x) & (y == root_y)
+    straight = root_x == 0
 
     barrier = pltpu.get_barrier_semaphore()
     for where in (
@@ -145,23 +147,24 @@
 
     step = rows // 8
     load_inverse.wait()
-    mine = inverse_rows[pl.ds(pl.multiple_of(grid * share, share), share), :]
+    pair_at = jnp.where(team == 0, x, y)
+    mine = inverse_rows[pl.ds(pl.multiple_of(pair_at * share, share), share), :]
     rounded = mine.astype(jnp.bfloat16)
-    row_at = lax.broadcasted_iota(jnp.int32, mine.shape, 0) + (team * side + z * width + grid * share)
+    row_at = lax.broadcasted_iota(jnp.int32, mine.shape, 0) + (team * side + z * width + pair_at * share)
     on_diagonal = lax.broadcasted_iota(jnp.int32, mine.shape, 1) == row_at
     rest = jnp.sum(jnp.where(on_diagonal, mine - rounded.astype(jnp.float32), 0.0), axis=1, keepdims=True)
     rest = jnp.broadcast_to(rest, (share, inv_diag.shape[4] - side)).astype(jnp.bfloat16)
 
     @pl.when(team == 0)
     def _():
-        inv_diag[0, z, grid, :, :side] = rounded[:, :side]
+        inv_diag[0, z, pair_at, :, :side] = rounded[:, :side]
 
     @pl.when(team == 1)
     def _():
-        inv_diag[1, z, grid, :, :side] = rounded[:, side:]
-        inv_off[z, grid] = rounded[:, :side]
-
-    inv_diag[team, z, grid, :, side:] = rest
+        inv_diag[1, z, pair_at, :, :side] = rounded[:, side:]
+        inv_off[z, pair_at] = rounded[:, :side]
+
+    inv_diag[team, z, pair_at, :, side:] = rest
 
     pl.semaphore_wait(barrier, jnp.where(is_inner, 9, 8))
 
@@ -201,38 +204,30 @@
                 if what == "start":
                     @pl.when(has & sends)
                     def _():
-                        ref = of(jnp.clip(held, 0, lines - 1), grid)
+                        ref = of(jnp.clip(held, 0, lines - 1), pair_at)
                         remote(ref, ref, inv_line_send.at[k, d, s], inv_line_recv.at[k, d, s],
                                {"obs": jnp.clip(z + hop, 0, lines - 1)}).start()
                 elif what == "wait":
                     @pl.when(has & comes)
                     def _():
-                        await_on(of(jnp.clip(came, 0, lines - 1), grid), inv_line_recv.at[k, d, s])
+                        await_on(of(jnp.clip(came, 0, lines - 1), pair_at), inv_line_recv.at[k, d, s])
                 else:
                     @pl.when(has & sends)
                     def _():
-                        await_on(of(jnp.clip(held, 0, lines - 1), grid), inv_line_send.at[k, d, s])
-
-    def inv_grid(stage, what):
-        every, first, last = pl.ds(0, lines), pl.ds(0, lines // 2), pl.ds(lines // 2, lines // 2)
+                        await_on(of(jnp.clip(held, 0, lines - 1), pair_at), inv_line_send.at[k, d, s])
+
+    def inv_grid(what):
+        every = pl.ds(0, lines)
         for k, has, of in inv_parts:
-            moves = (
-                (0, (every, grid), (every, beside_x), {"grid": beside_x}),
-                (1, (every, grid), (every, beside_y), {"grid": beside_y}),
-            ) if stage == 0 else (
-                (2, (first, beside_x), (first, across), {"grid": beside_y}),
-                (3, (last, beside_y), (last, across), {"grid": beside_x}),
-            )
-
             @pl.when(has)
             def _():
-                for j, sent, came, where in moves:
-                    if what == "start":
-                        remote(of(*sent), of(*sent), inv_grid_send.at[k, j], inv_grid_recv.at[k, j], where).start()
-                    elif what == "wait":
-                        await_on(of(*came), inv_grid_recv.at[k, j])
-                    else:
-                        await_on(of(*sent), inv_grid_send.at[k, j])
+                sent, came = of(every, pair_at), of(every, 1 - pair_at)
+                if what == "start":
+                    remote(sent, sent, inv_grid_send.at[k], inv_grid_recv.at[k], {"grid": first}).start()
+                elif what == "wait":
+                    await_on(came, inv_grid_recv.at[k])
+                else:
+                    await_on(sent, inv_grid_send.at[k])
 
     def inv_team(what):
         for k, has, of in inv_parts:
@@ -310,6 +305,10 @@
     def in_half(c):
         return half == c // side_pieces
 
+    def relays(u):
+        stored = at_x & in_half(UNITS[u][1])
+        return stored & jnp.logical_not(straight) if u >= DIRECT else stored
+
     def compute(u):
         r, c = UNITS[u]
         if r == 0:
@@ -345,7 +344,9 @@
             remote(ref, to, tile_send.at[0, k], tile_recv.at[team, k], {"team": owner, "grid": beside_x}).start()
             remote(ref, to, tile_send.at[1, k], tile_recv.at[team, k], {"team": owner, "grid": beside_y}).start()
             if u >= DIRECT:
-                remote(ref, to, tile_send.at[3, k], tile_recv.at[team, k], {"team": owner, "grid": across}).start()
+                @pl.when(straight)
+                def _():
+                    remote(ref, to, tile_send.at[3, k], tile_recv.at[team, k], {"team": owner, "grid": across}).start()
 
             @pl.when(team == owner)
             def _():
@@ -380,7 +381,7 @@
         r, c = UNITS[u]
         k = slot_of(r, c)
 
-        @pl.when(at_x & in_half(c))
+        @pl.when(relays(u))
         def _():
             for t in (0, 1):
                 ref = tile.at[tile_place(t, r, c)]
@@ -392,49 +393,56 @@
     blocks = blk.shape[1] // size
     pair = team * lines + z
 
-    def factor_of(ref, c, r):
-        t, inner = r * size // side, r * size % side
-        begin, near = inner // slab, slice(r * size, (r + 1) * size)
-        ahead = inv_diag[t, begin:begin + 2].reshape((size, inv_diag.shape[4]))
-        total = ahead[:, side:side + 1].astype(jnp.float32) * ref[c, near].astype(jnp.float32)
+    def factor_of(ref, c, t):
+        middle_row, begin = side // 2, t * side
+        near = inv_diag[t].reshape((side, inv_diag.shape[4]))
+        total = near[:, side:side + 1].astype(jnp.float32) * ref[c, begin:begin + side].astype(jnp.float32)
         total += jnp.dot(
-            ahead[:, :inner + size], ref[c, t * side:t * side + inner + size],
+            near[:, :middle_row], ref[c, begin:begin + middle_row], preferred_element_type=jnp.float32
+        )
+        if t:
+            total += jnp.dot(
+                inv_off[...].reshape((side, side)), ref[c, :side], preferred_element_type=jnp.float32
+            )
+        lower = total[middle_row:] + jnp.dot(
+            near[middle_row:, middle_row:side], ref[c, begin + middle_row:begin + side],
             preferred_element_type=jnp.float32,
         )
-        if t:
-            behind = inv_off[begin:begin + 2].reshape((size, side))
-            total += jnp.dot(behind, ref[c, :side], preferred_element_type=jnp.float32)
-        return total
+        return total[:middle_row], lower
 
     def factor_columns(c, r):
         if r == 0:
             for u in range(len(UNITS)):
                 if UNITS[u][1] == c:
                     await_on(blk.at[place(partner, *UNITS[u])], team_recv.at[u])
-        value = factor_of(blk, c, r)
-        cols[c, r * size:(r + 1) * size] = value.astype(jnp.bfloat16)
-        for part in range(size // slab):
-            @pl.when(pair == r * (size // slab) + part)
-            def _():
-                factor_part[:, c * wide:(c + 1) * wide] = value[part * slab:(part + 1) * slab]
+        if r % 2 == 0:
+            return
+        for k, value in enumerate(factor_of(blk, c, r // 2), r - 1):
+            cols[c, k * size:(k + 1) * size] = value.astype(jnp.bfloat16)
+            for part in range(size // slab):
+                @pl.when(pair == k * (size // slab) + part)
+                def _():
+                    factor_part[:, c * wide:(c + 1) * wide] = value[part * slab:(part + 1) * slab]
 
     def factor_tile(j, r):
         if r == 0:
             for u, (d, c) in enumerate(UNITS):
                 if c % side_pieces == j:
-                    @pl.when(in_half(c) & (jnp.logical_not(at_x) | (u >= DIRECT)))
+                    @pl.when(in_half(c) & jnp.logical_not(relays(u)))
                     def _():
                         for t in (0, 1):
                             await_on(tile.at[tile_place(t, d, c)], tile_recv.at[t, slot_of(d, c)])
-        value = factor_of(tile, j, r)
-        upper = value.astype(jnp.bfloat16)
-        high[j, r * size:(r + 1) * size] = upper
-        low[j, r * size:(r + 1) * size] = (value - upper.astype(jnp.float32)).astype(jnp.bfloat16)
+        if r % 2 == 0:
+            return
+        for k, value in enumerate(factor_of(tile, j, r // 2), r - 1):
+            upper = value.astype(jnp.bfloat16)
+            both[j, k * size:(k + 1) * size, :wide] = upper
+            both[j, k * size:(k + 1) * size, wide:] = (value - upper.astype(jnp.float32)).astype(jnp.bfloat16)
 
     def update(c, j):
         near, at = slice(j * wide, (j + 1) * wide), slice(c * wide, (c + 1) * wide)
-        change = contract_rows(high[j], cols[c]) + contract_rows(low[j], cols[c])
-        held[near, at] = held[near, at] - change
+        change = contract_rows(both[j], cols[c])
+        held[near, at] = held[near, at] - (change[:wide] + change[wide:])
 
     last = len(UNITS)
     work = [(compute, (u,)) for u in range(last)]
@@ -458,33 +466,30 @@
     def hooks(i):
         if i == 0:
             load_panel.wait()
-        if i == 2:
+        if i == 3:
+            panel_copies[1].start()
             inv_line(0, "wait")
             inv_line(1, "start")
-        if i == 4:
+        if i == starts[1]:
+            panel_copies[0].wait_recv()
+            panel_copies[2].start()
+        if i == starts[1] + 1:
             inv_line(1, "wait")
             inv_line(2, "start")
-        if i == 3:
-            panel_copies[1].start()
-        if i == starts[1]:
-            inv_line(2, "wait")
-            panel_copies[0].wait_recv()
-            panel_copies[2].start()
         if i == starts[2]:
             panel_copies[1].wait_recv()
             panel_copies[3].start()
-            inv_grid(0, "start")
+        if i == starts[2] + 2:
+            inv_line(2, "wait")
+            inv_grid("start")
         if i == starts[3]:
             panel_copies[2].wait_recv()
             panel_copies[3].wait_recv()
         if i == early:
             for u in range(count):
                 spread_tile(u)
-        if i == starts[3] + 5:
-            inv_grid(0, "wait")
-            inv_grid(1, "start")
-        if i == starts[3] + 8:
-            inv_grid(1, "wait")
+        if i == last - 1:
+            inv_grid("wait")
             inv_team("start")
         if i == last:
             inv_team("wait")
@@ -516,8 +521,7 @@
         copy.wait_send()
     for s in range(lines - 1):
         inv_line(s, "drain")
-    inv_grid(0, "drain")
-    inv_grid(1, "drain")
+    inv_grid("drain")
     inv_team("drain")
     for u in range(last):
         r, c = UNITS[u]
@@ -540,21 +544,22 @@
             await_on(ref, tile_send.at[0, k])
             await_on(ref, tile_send.at[1, k])
             if u >= DIRECT:
-                await_on(ref, tile_send.at[3, k])
+                @pl.when(straight)
+                def _():
+                    await_on(ref, tile_send.at[3, k])
 
             @pl.when(team != owner)
             def _():
                 await_on(ref, tile_send.at[2, k])
 
-        if u < DIRECT:
-            @pl.when(in_half(c) & at_x)
-            def _():
-                for t in (0, 1):
-                    await_on(tile.at[tile_place(t, r, c)], relay_send.at[t, k])
-
-
-def finish(cols, high, low, held, factor_part, factor_out, front_out, done, sems):
-    count, side_pieces = cols.shape[0], high.shape[0]
+        @pl.when(relays(u))
+        def _():
+            for t in (0, 1):
+                await_on(tile.at[tile_place(t, r, c)], relay_send.at[t, k])
+
+
+def finish(cols, both, held, factor_part, factor_out, front_out, done, sems):
+    count, side_pieces = cols.shape[0], both.shape[0]
     wide = cols.shape[2]
     near = (side_pieces - 1) * wide
     copies = [pltpu.make_async_copy(factor_part, factor_out, sems.at[0])]
@@ -565,8 +570,8 @@
 
     def update(j, c):
         rows, columns = slice(j * wide, (j + 1) * wide), slice(c * wide, (c + 1) * wide)
-        change = contract_rows(high[j], cols[c]) + contract_rows(low[j], cols[c])
-        done[rows, columns] = held[rows, columns] - change
+        change = contract_rows(both[j], cols[c])
+        done[rows, columns] = held[rows, columns] - (change[:wide] + change[wide:])
         at = (pl.ds(j * wide, wide), pl.ds(c * wide, wide))
         copies.append(pltpu.make_async_copy(done.at[at], front_out.at[at], sems.at[len(copies)]))
         copies[-1].start()
@@ -586,7 +591,7 @@
     cols = design_front.shape[1]
     tile_rows = front.shape[0]
     side = whole // 2
-    share = slab // grids
+    share = slab // 2
     wide = tile_rows // 3
     count = cols // wide
     vmem = pl.BlockSpec(memory_space=pltpu.VMEM)
@@ -606,18 +611,17 @@
         exchange,
         out_shape=(
             jax.ShapeDtypeStruct((count, whole, wide), bf16),
-            jax.ShapeDtypeStruct((3, whole, wide), bf16),
-            jax.ShapeDtypeStruct((3, whole, wide), bf16),
+            jax.ShapeDtypeStruct((3, whole, 2 * wide), bf16),
             jax.ShapeDtypeStruct(front.shape, f32),
             jax.ShapeDtypeStruct((slab, cols), f32),
         ),
         in_specs=[hbm, hbm, hbm, hbm, smem, hbm, hbm],
-        out_specs=(vmem,) * 5,
+        out_specs=(vmem,) * 4,
         scratch_shapes=[
             pltpu.VMEM((count, whole, wide), bf16),
             pltpu.VMEM((3, whole, wide), bf16),
-            pltpu.VMEM((2, lines, grids, share, side + 128), bf16),
-            pltpu.VMEM((lines, grids, share, side), bf16),
+            pltpu.VMEM((2, lines, 2, share, side + 128), bf16),
+            pltpu.VMEM((lines, 2, share, side), bf16),
             pltpu.VMEM((rows // arcs, arcs), jnp.int32),
             pltpu.VMEM((1, arcs), f32),
             pltpu.VMEM((slab, whole), f32),
@@ -632,7 +636,7 @@
             dma((units,)), dma((units,)), dma((units,)), dma((units,)),
             dma((units,)), dma((units,)), dma((units,)), dma((units,)),
             dma((4, slots)), dma((2, slots)), dma((2, slots)),
-            dma((3, 2, hops)), dma((3, 2, hops)), dma((3, 4)), dma((3, 4)), dma((3,)), dma((3,)),
+            dma((3, 2, hops)), dma((3, 2, hops)), dma((3,)), dma((3,)), dma((3,)), dma((3,)),
         ],
         compiler_params=pltpu.CompilerParams(
             collective_id=0, has_side_effects=True, vmem_limit_bytes=30 * 2**20
@@ -646,7 +650,7 @@
             jax.ShapeDtypeStruct((slab, cols), f32),
             jax.ShapeDtypeStruct(front.shape, f32),
         ),
-        in_specs=[vmem] * 5,
+        in_specs=[vmem] * 4,
         out_specs=(hbm, hbm),
         scratch_shapes=[
             pltpu.VMEM(front.shape, f32),

time: 71.4 us -> 71.5 us (level)
  no operation moved by 1% of the time
where the time goes in v5:
time: 71.5 us; the launch traced here: 71.3 us
  Pallas kernels  69.9 us (98%)
  between operations  1.45 us (2%)
    pallas_call x1, Pallas kernels, local_kernels(): pl.pallas_call(exchange, out_shape=(jax.ShapeDtypeStruct((count, whole, w...  66.5 us
    pallas_call x1, Pallas kernels, local_kernels(): pl.pallas_call(finish, out_shape=(jax.ShapeDtypeStruct((slab, cols), f32)...  3.36 us

profile of v5, /device:TPU:0, one launch (start us, length us, event | category | flops | bytes accessed | tf_op | source)
XLA Modules:
  0.0 71.3 jit_solution(11161692390852067503)
XLA Ops:
  1.3 66.5 %exchange.1 = (bf16[6,1024,256]{2,1,0:T(8,128)(2,1)S(1)}, bf16[3,1024,512]{2,1,0:T(8,128)(2,1)S(1)}, f32[768,1536]{1,0:T(8,128)S(1)}, f32[128,1536]{1,0:T(8,128)S(1)}) custom-call(bf16[2048,128]{1,0:T(8,128)(2,1)} %panel.1, bf16[2048,1536]{1,0:T(8,128)(2,1)} %front_cols.1, s32[16,128]{1,0:T(8,128)} %bitcast.2, f32[1,128]{1,0:T(1,128)} %bitcast.3, ...), custom_call_target="tpu_custom_call" | custom-call | tf_op jit(solution)/shard_map/exchange/pallas_call | solution.py:610
  67.8 3.4 %finish.1 = (f32[128,1536]{1,0:T(8,128)}, f32[768,1536]{1,0:T(8,128)}) custom-call(bf16[6,1024,256]{2,1,0:T(8,128)(2,1)S(1)} %get-tuple-element.6.cols, bf16[3,1024,512]{2,1,0:T(8,128)(2,1)S(1)} %get-tuple-element.7.both, f32[768,1536]{1,0:T(8,128)S(1)} %get-tuple-element.8.held, f32[128,1536]{1,0:T(8,128)S(1)} %get-tuple-element.9.factor_part), custom_call_target="tpu_custom_call" | custom-call | tf_op jit(solution)/shard_map/finish/pallas_call | solution.py:647

commit v6 on v5

--- a/solution.py
+++ b/solution.py
@@ -61,23 +61,23 @@
     (2, 4), (3, 0), (3, 3), (3, 1), (3, 4), (1, 2), (2, 2), (3, 2), (1, 5), (2, 5), (3, 5)
 )
 INNER = (
-    (0, 0, 4), (0, 1, 5), (0, 2, 6), (0, 3, 8), (1, 0, 8), (0, 4, 9), (1, 1, 9), (0, 5, 10), (1, 2, 10), (0,
-    6, 10), (1, 3, 11), (0, 7, 12), (1, 4, 12), (0, 8, 14), (1, 5, 14), (0, 9, 14), (1, 6, 14), (0, 10, 14),
-    (1, 7, 14), (0, 11, 15), (1, 8, 15), (0, 12, 16), (1, 9, 17), (0, 13, 18), (1, 10, 18), (0, 14, 19), (1,
-    11, 20), (2, 0, 20), (2, 1, 20), (0, 15, 21), (1, 12, 21), (2, 2, 21), (2, 3, 21), (0, 16, 22), (1, 13,
-    22), (2, 4, 22), (2, 5, 22), (0, 17, 23), (1, 14, 23), (2, 6, 24), (0, 18, 24), (2, 7, 24), (1, 15, 24),
-    (2, 8, 25), (2, 9, 25), (0, 19, 27), (1, 16, 28), (2, 10, 28), (2, 11, 28), (0, 20, 30), (1, 17, 31), (2,
-    12, 31), (2, 13, 31), (0, 21, 32), (1, 18, 34), (2, 14, 35), (2, 15, 35), (0, 22, 36), (1, 19, 37), (2,
-    16, 39), (2, 18, 39), (0, 23, 40), (1, 20, 40), (2, 17, 40), (1, 21, 40), (1, 22, 40), (2, 19, 42), (1,
+    (0, 0, 5), (0, 1, 6), (0, 2, 6), (0, 3, 8), (0, 4, 10), (1, 0, 10), (0, 5, 10), (1, 1, 10), (0, 6, 11),
+    (1, 2, 11), (0, 7, 12), (1, 3, 12), (0, 8, 14), (1, 4, 14), (0, 9, 14), (1, 5, 14), (0, 10, 14), (1, 6,
+    14), (0, 11, 15), (1, 7, 15), (0, 12, 17), (1, 8, 17), (0, 13, 18), (1, 9, 18), (0, 14, 20), (1, 10, 20),
+    (2, 0, 21), (0, 15, 21), (1, 11, 21), (2, 1, 21), (2, 2, 22), (2, 3, 22), (0, 16, 22), (1, 12, 22), (2, 4,
+    23), (2, 5, 23), (0, 17, 24), (1, 13, 24), (2, 6, 24), (2, 7, 24), (0, 18, 24), (1, 14, 24), (2, 8, 24),
+    (2, 9, 24), (0, 19, 24), (1, 15, 24), (2, 10, 27), (2, 11, 27), (0, 20, 28), (1, 16, 28), (2, 12, 29), (0,
+    21, 31), (1, 17, 31), (2, 13, 31), (2, 14, 34), (0, 22, 35), (1, 18, 35), (2, 15, 37), (0, 23, 38), (1,
+    19, 38), (2, 16, 40), (1, 20, 40), (2, 17, 40), (1, 21, 40), (1, 22, 40), (2, 18, 40), (2, 19, 43), (1,
     23, 45), (2, 20, 45), (2, 21, 45), (2, 22, 45), (2, 23, 50)
 )
 OUTER = (
-    (1, 0, 12), (1, 1, 14), (1, 2, 14), (1, 3, 14), (1, 4, 14), (1, 5, 17), (1, 6, 19), (1, 7, 21), (2, 0,
-    22), (2, 1, 22), (1, 8, 22), (2, 2, 24), (2, 3, 24), (1, 9, 24), (2, 4, 24), (2, 5, 24), (1, 10, 24), (2,
-    6, 24), (2, 7, 24), (1, 11, 24), (2, 8, 24), (1, 12, 24), (2, 9, 24), (1, 13, 24), (2, 10, 24), (1, 14,
-    24), (2, 11, 24), (1, 15, 24), (2, 12, 26), (1, 16, 29), (2, 13, 30), (1, 17, 32), (2, 14, 34), (1, 18,
-    37), (2, 15, 38), (1, 19, 40), (2, 16, 40), (1, 20, 40), (2, 17, 40), (1, 21, 40), (2, 18, 42), (1, 22,
-    44), (2, 19, 45), (2, 20, 45), (2, 21, 45), (1, 23, 46), (2, 22, 49), (2, 23, 51)
+    (1, 0, 14), (1, 1, 14), (1, 2, 14), (1, 3, 15), (1, 4, 18), (1, 5, 20), (1, 6, 22), (2, 0, 23), (2, 1,
+    23), (1, 7, 23), (2, 2, 24), (2, 3, 24), (1, 8, 24), (2, 4, 24), (2, 5, 24), (1, 9, 24), (2, 6, 24), (1,
+    10, 24), (2, 7, 24), (1, 11, 24), (2, 8, 24), (1, 12, 24), (2, 9, 24), (1, 13, 24), (2, 10, 24), (1, 14,
+    24), (2, 11, 24), (1, 15, 24), (2, 12, 27), (1, 16, 29), (2, 13, 32), (1, 17, 32), (2, 14, 35), (1, 18,
+    37), (2, 15, 40), (1, 19, 40), (2, 16, 40), (1, 20, 40), (2, 17, 40), (1, 21, 40), (1, 22, 40), (2, 18,
+    42), (1, 23, 44), (2, 19, 45), (2, 20, 45), (2, 21, 45), (2, 22, 45), (2, 23, 49)
 )
 
 

time: 71.5 us -> 71.2 us (level)
  no operation moved by 1% of the time
where the time goes in v6:
time: 71.2 us; the launch traced here: 71 us
  Pallas kernels  69.6 us (98%)
  between operations  1.45 us (2%)
    pallas_call x1, Pallas kernels, local_kernels(): pl.pallas_call(exchange, out_shape=(jax.ShapeDtypeStruct((count, whole, w...  66.2 us
    pallas_call x1, Pallas kernels, local_kernels(): pl.pallas_call(finish, out_shape=(jax.ShapeDtypeStruct((slab, cols), f32)...  3.36 us

profile of v6, /device:TPU:0, one launch (start us, length us, event | category | flops | bytes accessed | tf_op | source)
XLA Modules:
  0.0 71.0 jit_solution(1046341687937205955)
XLA Ops:
  1.3 66.2 %exchange.1 = (bf16[6,1024,256]{2,1,0:T(8,128)(2,1)S(1)}, bf16[3,1024,512]{2,1,0:T(8,128)(2,1)S(1)}, f32[768,1536]{1,0:T(8,128)S(1)}, f32[128,1536]{1,0:T(8,128)S(1)}) custom-call(bf16[2048,128]{1,0:T(8,128)(2,1)} %panel.1, bf16[2048,1536]{1,0:T(8,128)(2,1)} %front_cols.1, s32[16,128]{1,0:T(8,128)} %bitcast.2, f32[1,128]{1,0:T(1,128)} %bitcast.3, ...), custom_call_target="tpu_custom_call" | custom-call | tf_op jit(solution)/shard_map/exchange/pallas_call | solution.py:610
  67.5 3.4 %finish.1 = (f32[128,1536]{1,0:T(8,128)}, f32[768,1536]{1,0:T(8,128)}) custom-call(bf16[6,1024,256]{2,1,0:T(8,128)(2,1)S(1)} %get-tuple-element.6.cols, bf16[3,1024,512]{2,1,0:T(8,128)(2,1)S(1)} %get-tuple-element.7.both, f32[768,1536]{1,0:T(8,128)S(1)} %get-tuple-element.8.held, f32[128,1536]{1,0:T(8,128)S(1)} %get-tuple-element.9.factor_part), custom_call_target="tpu_custom_call" | custom-call | tf_op jit(solution)/shard_map/finish/pallas_call | solution.py:647
